TPU v7x, 512 devices: a whole 4x8x8 slice. The times are simulated.
512 devices in a mesh: lat: 32 (over x, z), lev: 16 (over y, core).
Axes of the slice: x: 4, y: 8, z: 8, core: 2. Of those that a mesh axis runs over, the one named last changes fastest.
Arguments:
- fields: float32 [2, 128, 64, 3072], P(None, 'lat', 'lev'), may hold values from -6 to 6
- courant: bfloat16 [2, 128, 64, 3072], P(None, 'lat', 'lev'), may hold values from -0.3984375 to 0.3984375
- cutoffs: int32 [128], replicated, may hold values from 1 to 1536, as said below
- surface: float32 [128, 3072], P('lat'), may hold values from -6 to 6
- remap_weights: float32 [64, 64], replicated, may hold values from -0.25 to 0.75
Outputs:
- remapped: float32 [2, 128, 64, 3072], P(None, 'lat', None, 'lev')
- geopotential: float32 [128, 64, 3072], P('lat', None, 'lev')
Inputs may be any that keep to these rules, and one draw needn't show every extreme that they name: cutoffs[j] is 1536 except on the first and the last 16 latitudes, where it lies between 1 and 127; it equals 127 on some latitude among the first 16.
All inputs are finite; a program needn't handle non-finite values.
Results may differ from a plain program's by a relative error of at most 0.0003.
Values may be sent and summed in bfloat16 or wider, within the bound.
A program may use at most 64 MiB of HBM per device.

v0:
```python
import math

import jax
import jax.numpy as jnp
from jax import lax
from jax.sharding import PartitionSpec as P

KMAX = 128


def with_halo(shard, sides, width):
    for axis, dim in sides:
        size, length = (lax.axis_size(axis), shard.shape[dim])
        up = [(i, (i + 1) % size) for i in range(size - 1)]
        down = [(j, i) for i, j in up]
        last = lax.slice_in_dim(shard, length - width, length, axis=dim)
        leading = lax.slice_in_dim(shard, 0, width, axis=dim)
        before = lax.ppermute(last, axis, up)
        after = lax.ppermute(leading, axis, down)
        shard = jnp.concatenate([before, shard, after], axis=dim)
    return shard


def entering(part, axis, combine, identity):
    count = lax.axis_size(axis)
    place = lax.axis_index(axis)
    ahead = count - 1 - place
    gathered = lax.all_gather(part, axis)
    state = jnp.zeros_like(part) + jnp.asarray(identity, part.dtype)

    def one(lap, state):
        source = count - 1 - lap
        return combine(state, lax.dynamic_index_in_dim(gathered, source, 0, False))

    return lax.fori_loop(0, ahead, one, state)


def lon_part(values, east_wind):
    interface = (
        7.0 * (values + jnp.roll(values, -1, -1))
        - (jnp.roll(values, 1, -1) + jnp.roll(values, -2, -1))
    ) / 12.0
    face_wind = 0.5 * (east_wind + jnp.roll(east_wind, -1, -1))
    flux_faces = face_wind * interface
    return flux_faces - jnp.roll(flux_faces, 1, -1)


def lat_part(padded, north_wind):
    row_count = padded.shape[1] - 4
    interface = (
        7.0 * (padded[:, 1 : row_count + 2] + padded[:, 2 : row_count + 3])
        - (padded[:, 0 : row_count + 1] + padded[:, 3 : row_count + 4])
    ) / 12.0
    face_wind = 0.5 * (north_wind[0 : row_count + 1] + north_wind[1 : row_count + 2])
    flux_faces = face_wind * interface
    return flux_faces[:, 1:] - flux_faces[:, :-1]


def advance(padded, east_wind, north_wind):
    middle = padded[:, 2:-2]
    return middle - lon_part(middle, east_wind) - lat_part(padded, north_wind)


def spectral_tables(length, wave_count):
    wave_numbers = jnp.arange(wave_count, dtype=jnp.int32)
    points = jnp.arange(length, dtype=jnp.int32)
    phase = points[:, None] * wave_numbers[None, :] % length
    angle = phase.astype(jnp.float32) * (2.0 * math.pi / length)
    return (jnp.cos(angle), jnp.sin(angle))


def polar_filter(values, cutoff_rows, cosine_table, sine_table):
    length = values.shape[-1]
    wave_count = cosine_table.shape[1]
    flagged = cutoff_rows < length // 2

    def smooth(inputs):
        real_part = jnp.einsum(
            "frln,nk->frlk", inputs, cosine_table, precision=lax.Precision.HIGHEST
        )
        imag_part = jnp.einsum("frln,nk->frlk", inputs, sine_table, precision=lax.Precision.HIGHEST)
        wave_numbers = jnp.arange(wave_count, dtype=jnp.int32)
        doubled = jnp.where(wave_numbers == 0, 1.0, 2.0).astype(jnp.float32)
        weight = (
            jnp.where(wave_numbers[None, :] <= cutoff_rows[:, None], doubled[None, :], 0.0) / length
        )
        weight = weight[None, :, None, :]
        lowpass = jnp.einsum(
            "frlk,nk->frln", real_part * weight, cosine_table, precision=lax.Precision.HIGHEST
        )
        lowpass = lowpass + jnp.einsum(
            "frlk,nk->frln", imag_part * weight, sine_table, precision=lax.Precision.HIGHEST
        )
        return jnp.where(flagged[None, :, None, None], lowpass, inputs)

    return lax.cond(jnp.any(flagged), smooth, lambda inputs: inputs, values)


def upward_matrix(count):
    levels = jnp.arange(count, dtype=jnp.int32)
    deeper = (levels[None, :] > levels[:, None]).astype(jnp.float32)
    same_level = (levels[None, :] == levels[:, None]).astype(jnp.float32)
    return deeper + 0.5 * same_level


def shards(fields, courant, cutoffs, surface, remap_weights):
    band_rows = fields.shape[1]
    length = fields.shape[-1]
    nyquist = length // 2
    first_row = lax.axis_index("lat") * band_rows
    padded_cut = jnp.pad(cutoffs, 2, constant_values=nyquist)
    own_cut = lax.dynamic_slice_in_dim(padded_cut, first_row + 2, band_rows)
    cosine_table, sine_table = spectral_tables(length, KMAX)
    rim_depth = 1
    winds_rimmed = with_halo(courant, (("lat", 1),), rim_depth).astype(jnp.float32)
    east_wind = winds_rimmed[0, 1:-1]
    north_wind = winds_rimmed[1]
    transported = fields
    for repeat in range(2):
        padded = with_halo(transported, (("lat", 1),), 2)
        transported = polar_filter(
            advance(padded, east_wind, north_wind), own_cut, cosine_table, sine_table
        )
    level_count = remap_weights.shape[0]
    geo_scale = level_count ** (-0.5)
    heat_rows = transported[1]
    own_total = jnp.sum(heat_rows, axis=1)
    deeper = entering(
        own_total, "lev", lambda earlier, later: earlier + later, jnp.zeros_like(own_total)
    )
    within = jnp.einsum(
        "kl,jln->jkn", upward_matrix(heat_rows.shape[1]), heat_rows, precision=lax.Precision.HIGHEST
    )
    geo_levels = surface[:, None, :] + geo_scale * (deeper[:, None, :] + within)
    packed = jnp.concatenate([transported, geo_levels[None]], axis=0)
    columns = lax.all_to_all(packed, "lev", split_axis=3, concat_axis=2, tiled=True)
    column_columns = columns[:2]
    remapped = jnp.einsum(
        "pk,fjkn->fjpn", remap_weights, column_columns, precision=lax.Precision.HIGHEST
    )
    geo_columns = columns[2:3]
    geopotential = geo_columns[0]
    return (remapped, geopotential)


def solution(mesh):
    return jax.shard_map(
        shards,
        mesh=mesh,
        in_specs=(
            P(None, "lat", "lev", None),
            P(None, "lat", "lev", None),
            P(),
            P("lat", None),
            P(),
        ),
        out_specs=(P(None, "lat", None, "lev"), P("lat", None, "lev")),
        check_vma=False,
    )
```

profile of v0, /device:TPU:1, one launch (start us, length us, event | category | flops | bytes accessed | tf_op | source)
XLA Modules:
  0.0 197.7 jit_solution(3813942538770517226)
XLA Ops:
  1.6 4.8 %collective-permute-start = (bf16[2,1,4,3072]{3,2,1,0:T(4,128)(2,1)S(1)}, bf16[2,1,4,3072]{3,2,1,0:T(4,128)(2,1)S(1)}, u32[]{:S(2)}, u32[]{:S(2)}) collective-permute-start(bf16[2,1,4,3072]{3,2,1,0:T(4,128)(2,1)S(1)} %get-tuple-element.130), channel_id=1, source_target_pairs={{0,16},{16,32},{32,48},{48,64},{64,80},{80,96},{96,112},{112,128},... | collective-permute-start | bytes 147464 | tf_op jit(solution)/shard_map/ppermute | solution.py:18
  6.4 1.3 collective-permute-start.1
  7.7 1.8 fusion.79
  9.5 5.3 %collective-permute-start.2 = (f32[2,2,4,3072]{3,2,1,0:T(4,128)}, f32[2,2,4,3072]{3,2,1,0:T(4,128)}, u32[]{:S(2)}, u32[]{:S(2)}) collective-permute-start(f32[2,2,4,3072]{3,2,1,0:T(4,128)} %get-tuple-element.128), channel_id=1, source_target_pairs={{0,16},{16,32},{32,48},{48,64},{64,80},{80,96},{96,112},{112,128},... | collective-permute-start | bytes 589832 | tf_op jit(solution)/shard_map/ppermute | solution.py:18
  14.8 1.3 collective-permute-start.3
  16.9 1.0 fusion.78
  17.9 7.2 %fusion.35 = (f32[3072,128]{1,0:T(8,128)S(1)}, f32[3072,128]{1,0:T(8,128)}) fusion(), kind=kLoop, calls=%fused_computation.39 | loop fusion | flops 3538944 | bytes 3145728 | tf_op jit(solution)/shard_map/sin | solution.py:69
  29.4 6.1 %conditional.2 = (f32[2,4,4,3072]{3,2,1,0:T(4,128)S(1)}) conditional(s32[]{:T(128)} %convert_element_type.28, f32[2,4,4,3072]{3,2,1,0:T(4,128)S(1)} %fusion.49, (pred[4]{0:T(512)(128)(4,1)S(1)}, f32[2,4,4,3072]{3,2,1,0:T(4,128)S(1)}, f32[3072,128]{1,0:T(8,128)}, s32[4]{0:T(128)S(1)}, f32[3072,128]{1,0:T(8,128)}, /*index=5*/f32[3072,128]{1,0:T(8,128)S(1)}, ...), branch_computations={%region_1.2_spmd, %region_2.3_spmd} | conditional | flops 604186368 | bytes 15014968 | solution.py:96
  29.6 1.1 fusion.11
  30.9 1.1 fusion.8
  32.0 1.7 fusion.4
  33.7 1.8 fusion
  36.2 4.0 %collective-permute-start.4 = (f32[2,2,4,3072]{3,2,1,0:T(4,128)S(1)}, f32[2,2,4,3072]{3,2,1,0:T(4,128)S(1)}, u32[]{:S(2)}, u32[]{:S(2)}) collective-permute-start(f32[2,2,4,3072]{3,2,1,0:T(4,128)S(1)} %get-tuple-element.119), channel_id=1, source_target_pairs={{0,16},{16,32},{32,48},{48,64},{64,80},{80,96},{96,112},{112,128},... | collective-permute-start | bytes 589832 | tf_op jit(solution)/shard_map/ppermute | solution.py:18
  40.2 1.3 collective-permute-start.5
  42.8 5.6 %collective-permute-done.5 = f32[2,2,4,3072]{3,2,1,0:T(4,128)S(1)} collective-permute-done((f32[2,2,4,3072]{3,2,1,0:T(4,128)S(1)}, f32[2,2,4,3072]{3,2,1,0:T(4,128)S(1)}, u32[]{:S(2)}, u32[]{:S(2)}) %collective-permute-start.5) | collective-permute-done | bytes 196640 | tf_op jit(solution)/shard_map/ppermute | solution.py:19
  48.6 1.0 fusion.48
  49.7 9.6 %conditional.3 = (f32[2,4,4,3072]{3,2,1,0:T(4,128)}) conditional(s32[]{:T(128)} %convert_element_type.28, f32[2,4,4,3072]{3,2,1,0:T(4,128)} %fusion.48, (pred[4]{0:T(512)(128)(4,1)S(1)}, f32[2,4,4,3072]{3,2,1,0:T(4,128)}, f32[3072,128]{1,0:T(8,128)}, s32[4]{0:T(128)S(1)}, f32[3072,128]{1,0:T(8,128)}, /*index=5*/f32[3072,128]{1,0:T(8,128)S(1)}, ...), branch_computations={%region_3.4_spmd, %region_4.5_spmd} | conditional | flops 604186368 | bytes 15014968 | solution.py:96
  49.8 2.2 %fusion.25 = f32[2,4,4,128]{3,2,1,0:T(4,128)S(1)} fusion(f32[2,4,4,3072]{3,2,1,0:T(4,128)} %get-tuple-element.89, f32[3072,128]{1,0:T(8,128)S(1)} %get-tuple-element.94, f32[4,128]{1,0:T(4,128)S(1)} %select_multiply_fusion.1), kind=kOutput, calls=%fused_computation.24 | convolution fusion | flops 150999040 | bytes 1984512 | tf_op jit(solution)/shard_map/cond/branch_1_fun/frln,nk->frlk/dot_general | solution.py:81
  52.0 2.1 %fusion.22 = f32[2,4,4,128]{3,2,1,0:T(4,128)S(1)} fusion(f32[2,4,4,3072]{3,2,1,0:T(4,128)} %get-tuple-element.89, f32[3072,128]{1,0:T(8,128)S(1)} %copy-done.2, f32[4,128]{1,0:T(4,128)S(1)} %select_multiply_fusion.1), kind=kOutput, calls=%fused_computation.23 | convolution fusion | flops 150999040 | bytes 1984512 | tf_op jit(solution)/shard_map/cond/branch_1_fun/frln,nk->frlk/dot_general | solution.py:78
  54.1 1.7 fusion.18
  55.8 3.5 %fusion.14 = f32[2,4,4,3072]{3,2,1,0:T(4,128)} fusion(f32[2,4,4,3072]{3,2,1,0:T(4,128)} %get-tuple-element.89, f32[2,4,4,3072]{3,2,1,0:T(4,128)S(1)} %fusion.18, f32[2,4,4,128]{3,2,1,0:T(4,128)S(1)} %fusion.25, f32[3072,128]{1,0:T(8,128)S(1)} %get-tuple-element.94, pred[4]{0:T(512)(128)(4,1)S(1)} %get-tuple-element.88), kind=kOutput, calls=%fused_computation.15 | convolution fusion | flops 151191552 | bytes 2768900 | tf_op jit(solution)/shard_map/cond/branch_1_fun/frlk,nk->frln/dot_general | solution.py:91
  59.3 1.0 slice_reduce_fusion
  60.3 22.4 %all-gather.1 = f32[16,4,3072]{2,1,0:T(4,128)S(1)} all-gather(f32[1,4,3072]{2,1,0:T(4,128)S(1)} %bitcast.101), channel_id=2, replica_groups=mesh['lat'=32,'lev'=16] {'lev'}, dimensions={0}, use_global_device_ids=true | all-gather | bytes 835584 | tf_op jit(solution)/shard_map/all_gather | solution.py:28
  83.5 1.4 fusion.30
  84.9 1.1 pad_maximum_fusion
  86.0 12.7 %copy.16 = f32[3,4,4,3072]{2,1,0,3:T(4,128)} copy(f32[3,4,4,3072]{3,2,1,0:T(4,128)S(1)} %pad_maximum_fusion) | data formatting | bytes 1179648 | tf_op jit(solution)/shard_map/concatenate | solution.py:135
  98.7 24.5 %reshape.111 = f32[16,1,9216]{2,1,0:T(1,128)S(1)} reshape(f32[3072,3,4,4]{3,2,1,0:T(4,128)} %bitcast.95) | data formatting | bytes 1179648
  123.2 22.8 %all_to_all.15 = f32[16,1,9216]{2,1,0:T(1,128)S(1)} all-to-all(f32[16,1,9216]{2,1,0:T(1,128)S(1)} %reshape.111), channel_id=1, replica_groups=mesh['lat'=32,'lev'=16] {'lev'}, dimensions={0} | all-to-all | bytes 1179648 | tf_op jit(solution)/shard_map/all_to_all | solution.py:136
  146.5 2.0 %reduce.1 = f32[16,9216]{1,0:T(8,128)S(1)} reduce(f32[16,1,9216]{2,1,0:T(1,128)S(1)} %all_to_all.15, f32[]{:T(128)} %broadcast.173), dimensions={1}, to_apply=%all_to_all.11.reduce_sub_computation | reduce | bytes 1179652 | tf_op jit(solution)/shard_map/all_to_all | solution.py:136
  148.6 31.6 %reshape.112 = f32[3072,3,4,4]{3,2,1,0:T(4,128)} reshape(f32[16,9216]{1,0:T(8,128)S(1)} %reduce.1) | data formatting | bytes 1179648
  180.2 15.1 %copy.17 = f32[3,4,4,16,192]{4,2,3,1,0:T(4,128)S(1)} copy(f32[3,4,4,16,192]{2,1,0,4,3:T(4,128)} %bitcast.96) | data formatting | bytes 1179648 | tf_op jit(solution)/shard_map/all_to_all | solution.py:136
  196.3 1.4 convolution_bitcast_fusion
  (73 shorter events, 10.4 us)
Async XLA Ops:
  0.6 195.7 %copy-start = (f32[64,64]{1,0:T(8,128)S(1)}, f32[64,64]{1,0:T(8,128)}, u32[]{:S(2)}) copy-start(f32[64,64]{1,0:T(8,128)} %param.15) | copy-start | bytes 49156
  0.6 16.3 %copy-start.3 = (f32[2,4,4,3072]{3,2,1,0:T(4,128)S(1)}, f32[2,4,4,3072]{3,2,1,0:T(4,128)}, u32[]{:S(2)}) copy-start(f32[2,4,4,3072]{3,2,1,0:T(4,128)} %param.11) | copy-start | bytes 1179652
  1.6 25.2 %collective-permute-start = (bf16[2,1,4,3072]{3,2,1,0:T(4,128)(2,1)S(1)}, bf16[2,1,4,3072]{3,2,1,0:T(4,128)(2,1)S(1)}, u32[]{:S(2)}, u32[]{:S(2)}) collective-permute-start(bf16[2,1,4,3072]{3,2,1,0:T(4,128)(2,1)S(1)} %get-tuple-element.130), channel_id=1, source_target_pairs={{0,16},{16,32},{32,48},{48,64},{64,80},{80,96},{96,112},{112,128},... | collective-permute-start | bytes 147464 | tf_op jit(solution)/shard_map/ppermute | solution.py:18
  6.4 20.4 %collective-permute-start.1 = (bf16[2,1,4,3072]{3,2,1,0:T(4,128)(2,1)S(1)}, bf16[2,1,4,3072]{3,2,1,0:T(4,128)(2,1)S(1)}, u32[]{:S(2)}, u32[]{:S(2)}) collective-permute-start(bf16[2,1,4,3072]{3,2,1,0:T(4,128)(2,1)S(1)} %get-tuple-element.131), channel_id=1, source_target_pairs={{16,0},{32,16},{48,32},{64,48},{80,64},{96,80},{112,96},{128,112},... | collective-permute-start | bytes 147464 | tf_op jit(solution)/shard_map/ppermute | solution.py:19
  9.5 17.9 %collective-permute-start.2 = (f32[2,2,4,3072]{3,2,1,0:T(4,128)}, f32[2,2,4,3072]{3,2,1,0:T(4,128)}, u32[]{:S(2)}, u32[]{:S(2)}) collective-permute-start(f32[2,2,4,3072]{3,2,1,0:T(4,128)} %get-tuple-element.128), channel_id=1, source_target_pairs={{0,16},{16,32},{32,48},{48,64},{64,80},{80,96},{96,112},{112,128},... | collective-permute-start | bytes 589832 | tf_op jit(solution)/shard_map/ppermute | solution.py:18
  14.8 14.1 %collective-permute-start.3 = (f32[2,2,4,3072]{3,2,1,0:T(4,128)}, f32[2,2,4,3072]{3,2,1,0:T(4,128)S(1)}, u32[]{:S(2)}, u32[]{:S(2)}) collective-permute-start(f32[2,2,4,3072]{3,2,1,0:T(4,128)} %get-tuple-element.129), channel_id=1, source_target_pairs={{16,0},{32,16},{48,32},{64,48},{80,64},{96,80},{112,96},{128,112},... | collective-permute-start | bytes 589832 | tf_op jit(solution)/shard_map/ppermute | solution.py:19
  17.9 7.2 %copy-start.7 = (s32[128]{0:T(128)S(1)}, s32[128]{0:T(128)}, u32[]{:S(2)}) copy-start(s32[128]{0:T(128)} %param.13) | copy-start | bytes 1540
  17.9 8.9 %copy-start.5 = (bf16[2,4,4,3072]{3,2,1,0:T(4,128)(2,1)S(1)}, bf16[2,4,4,3072]{3,2,1,0:T(4,128)(2,1)}, u32[]{:S(2)}) copy-start(bf16[2,4,4,3072]{3,2,1,0:T(4,128)(2,1)} %param.12) | copy-start | bytes 589828
  26.8 1.6 slice-start
  26.8 1.6 copy-start.4
  29.5 1.4 copy-start.1
  36.2 6.6 %collective-permute-start.4 = (f32[2,2,4,3072]{3,2,1,0:T(4,128)S(1)}, f32[2,2,4,3072]{3,2,1,0:T(4,128)S(1)}, u32[]{:S(2)}, u32[]{:S(2)}) collective-permute-start(f32[2,2,4,3072]{3,2,1,0:T(4,128)S(1)} %get-tuple-element.119), channel_id=1, source_target_pairs={{0,16},{16,32},{32,48},{48,64},{64,80},{80,96},{96,112},{112,128},... | collective-permute-start | bytes 589832 | tf_op jit(solution)/shard_map/ppermute | solution.py:18
  40.2 8.2 %collective-permute-start.5 = (f32[2,2,4,3072]{3,2,1,0:T(4,128)S(1)}, f32[2,2,4,3072]{3,2,1,0:T(4,128)S(1)}, u32[]{:S(2)}, u32[]{:S(2)}) collective-permute-start(f32[2,2,4,3072]{3,2,1,0:T(4,128)S(1)} %get-tuple-element.120), channel_id=1, source_target_pairs={{16,0},{32,16},{48,32},{64,48},{80,64},{96,80},{112,96},{128,112},... | collective-permute-start | bytes 589832 | tf_op jit(solution)/shard_map/ppermute | solution.py:19
  49.7 2.3 %copy-start.2 = (f32[3072,128]{1,0:T(8,128)S(1)}, f32[3072,128]{1,0:T(8,128)}, u32[]{:S(2)}) copy-start(f32[3072,128]{1,0:T(8,128)} %get-tuple-element.92) | copy-start | bytes 4718596 | tf_op jit(solution)/shard_map/cond
  59.3 24.2 %copy-start.6 = (f32[4,3072]{1,0:T(4,128)S(1)}, f32[4,3072]{1,0:T(4,128)}, u32[]{:S(2)}) copy-start(f32[4,3072]{1,0:T(4,128)} %param.14) | copy-start | bytes 147460
where the time goes:
time: 199 us; the launch traced here: 198 us
  local copies, waits for them, and re-layouts  92.4 us (46%)
  blocking collectives  45.2 us (23%)
  matrix products  18.1 us (9%)
  starting transfers between devices  18 us (9%)
  other arithmetic  15.6 us (8%)
  waiting for transfers between devices  6.48 us (3%)
    unnamed x15, local copies, waits for them, and re-layouts  57.1 us
    all_to_all x1, blocking collectives, shards(): lax.all_to_all(packed, 'lev', split_axis=3, concat_axis=2, tiled=True)  22.8 us
    all_gather x1, blocking collectives, entering(): gathered = lax.all_gather(part, axis)  22.4 us
    all_to_all x2, local copies, waits for them, and re-layouts, shards(): lax.all_to_all(packed, 'lev', split_axis=3, concat_axis=2, tiled=True)  15.6 us
    ppermute x3, starting transfers between devices, with_halo(): before = lax.ppermute(last, axis, up)  14.1 us
    concatenate x1, local copies, waits for them, and re-layouts, shards(): packed = jnp.concatenate([transported, geo_levels[None]], axis=0)  12.7 us
    sin x1, other arithmetic, spectral_tables(): return (jnp.cos(angle), jnp.sin(angle))  7.19 us
    ppermute x3, waiting for transfers between devices, with_halo(): after = lax.ppermute(leading, axis, down)  5.64 us
  transfers between devices with their start and end apart: 6, of which 2 were waited for; matrix products, arithmetic and copies ran while one was open for 7% of the time, Pallas kernels for 0%

commit v1 on v0

v1 whole, which is shorter than its diff:
```python
import functools

import jax
import jax.numpy as jnp
import numpy as np
from jax import lax
from jax.experimental import pallas as pl
from jax.experimental.pallas import tpu as pltpu
from jax.sharding import PartitionSpec as P

MESH = pl.DeviceIdType.MESH
KMAX = 128
SEG = 256
F32 = jnp.float32
BF16 = jnp.bfloat16


def split_bf16(table):
    high = table.astype(np.float32).astype(jnp.bfloat16)
    low = (table - high.astype(np.float64)).astype(np.float32).astype(jnp.bfloat16)
    return np.stack([high, low])


def fourier_tables(length):
    waves = np.arange(KMAX)
    phase = (np.arange(SEG)[:, None] * waves[None, :]) % length
    angle = phase * (2.0 * np.pi / length)
    inner = np.concatenate([np.cos(angle), np.sin(angle)], axis=1)
    segments = length // SEG
    outer = (np.arange(segments)[:, None] * waves[None, :]) % segments
    outer = outer * (2.0 * np.pi / segments)
    turn = np.stack([np.cos(outer), np.sin(outer)], axis=1).astype(np.float32)
    return split_bf16(inner), split_bf16(inner.T), turn.reshape(2 * segments, KMAX)


def halves(x):
    high = x.astype(BF16)
    return high, (x - high.astype(F32)).astype(BF16)


def dot3(x, high, low):
    x_high, x_low = halves(x)
    out = jnp.dot(x_high, high, preferred_element_type=F32)
    out += jnp.dot(x_low, high, preferred_element_type=F32)
    return out + jnp.dot(x_high, low, preferred_element_type=F32)


def zonal(u, coef):
    length = u.shape[-1]
    pair = u + pltpu.roll(u, length - 1, 1)
    face = 8.0 * pair - (pltpu.roll(pair, 1, 1) + pltpu.roll(pair, length - 1, 1))
    flux = coef * face
    return u - (flux - pltpu.roll(flux, 1, 1))


def kernel(
    n_lat, n_lev, polar,
    fields, courant, cutoffs, surface, weights, fwd, inv, turn,
    out, geo,
    cv, cut, surf, wv, fwd_v, inv_v, turn_v,
    u, z, coef_x, coef_y, halo, cy_halo, send, recv,
    in_sem, halo_send, halo_recv, cy_send, cy_recv, a2a_send, a2a_recv,
):
    ilat, ilev = lax.axis_index("lat"), lax.axis_index("lev")
    rows, length = u.shape[0], u.shape[2]
    levs = u.shape[1] // 2
    segments = length // SEG
    pair_id, parity = lax.div(ilev, 2), lax.rem(ilev, 2)
    width = 3 * 128

    loads = [
        pltpu.make_async_copy(fields.at[0], u.at[:, 0:levs, :], in_sem.at[0]),
        pltpu.make_async_copy(fields.at[1], u.at[:, levs : 2 * levs, :], in_sem.at[1]),
        pltpu.make_async_copy(courant, cv, in_sem.at[2]),
        pltpu.make_async_copy(cutoffs, cut, in_sem.at[3]),
        pltpu.make_async_copy(
            surface.at[:, pl.ds(pl.multiple_of(pair_id * width, 128), width)], surf, in_sem.at[4]
        ),
        pltpu.make_async_copy(weights, wv, in_sem.at[5]),
        pltpu.make_async_copy(fwd, fwd_v, in_sem.at[6]),
        pltpu.make_async_copy(inv, inv_v, in_sem.at[7]),
        pltpu.make_async_copy(turn, turn_v, in_sem.at[8]),
    ]
    for load in loads:
        load.start()

    has_minus, has_plus = ilat > 0, ilat < n_lat - 1
    barrier = pltpu.get_barrier_semaphore()

    @pl.when(has_minus)
    def _():
        pl.semaphore_signal(barrier, inc=1, device_id={"lat": ilat - 1}, device_id_type=MESH)

    @pl.when(has_plus)
    def _():
        pl.semaphore_signal(barrier, inc=1, device_id={"lat": ilat + 1}, device_id_type=MESH)

    @pl.loop(1, n_lev)
    def _(step):
        pl.semaphore_signal(
            barrier, inc=1, device_id={"lev": lax.rem(ilev + step, n_lev)}, device_id_type=MESH
        )

    for load in loads:
        load.wait()

    neighbours = has_minus.astype(jnp.int32) + has_plus.astype(jnp.int32)
    pl.semaphore_wait(barrier, n_lev - 1 + neighbours)

    def to_plus(phase):
        return pltpu.make_async_remote_copy(
            src_ref=u.at[rows - 2 : rows], dst_ref=halo.at[phase, 0],
            send_sem=halo_send.at[phase, 0], recv_sem=halo_recv.at[phase, 0],
            device_id={"lat": ilat + 1}, device_id_type=MESH,
        )

    def to_minus(phase):
        return pltpu.make_async_remote_copy(
            src_ref=u.at[0:2], dst_ref=halo.at[phase, 1],
            send_sem=halo_send.at[phase, 1], recv_sem=halo_recv.at[phase, 1],
            device_id={"lat": ilat - 1}, device_id_type=MESH,
        )

    def cy_plus():
        return pltpu.make_async_remote_copy(
            src_ref=cv.at[1, rows - 1], dst_ref=cy_halo.at[0],
            send_sem=cy_send.at[0], recv_sem=cy_recv.at[0],
            device_id={"lat": ilat + 1}, device_id_type=MESH,
        )

    def cy_minus():
        return pltpu.make_async_remote_copy(
            src_ref=cv.at[1, 0], dst_ref=cy_halo.at[1],
            send_sem=cy_send.at[1], recv_sem=cy_recv.at[1],
            device_id={"lat": ilat - 1}, device_id_type=MESH,
        )

    def both(x):
        return jnp.concatenate([x, x], axis=0)

    def exchange_start(phase):
        @pl.when(has_plus)
        def _():
            to_plus(phase).start()
            if phase == 0:
                cy_plus().start()

        @pl.when(has_minus)
        def _():
            to_minus(phase).start()
            if phase == 0:
                cy_minus().start()

        @pl.when(jnp.logical_not(has_minus))
        def _():
            halo[phase, 0] = jnp.zeros(halo.shape[2:], F32)
            if phase == 0:
                cy_halo[0] = jnp.zeros(cy_halo.shape[1:], BF16)

        @pl.when(jnp.logical_not(has_plus))
        def _():
            halo[phase, 1] = jnp.zeros(halo.shape[2:], F32)
            if phase == 0:
                cy_halo[1] = jnp.zeros(cy_halo.shape[1:], BF16)

    def exchange_wait(phase):
        @pl.when(has_minus)
        def _():
            to_plus(phase).wait_recv()
            to_minus(phase).wait_send()
            if phase == 0:
                cy_plus().wait_recv()
                cy_minus().wait_send()

        @pl.when(has_plus)
        def _():
            to_minus(phase).wait_recv()
            to_plus(phase).wait_send()
            if phase == 0:
                cy_minus().wait_recv()
                cy_plus().wait_send()

    def cy_row(j):
        if j < 0:
            return both(cy_halo[0].astype(F32))
        if j >= rows:
            return both(cy_halo[1].astype(F32))
        return both(cv[1, j].astype(F32))

    def meridional(phase):
        piece = 512

        @pl.loop(0, length // piece)
        def _(c):
            at = pl.ds(pl.multiple_of(c * piece, 128), piece)
            full = [halo[phase, 0, 0, :, at], halo[phase, 0, 1, :, at]]
            full += [u[j, :, at] for j in range(rows)]
            full += [halo[phase, 1, 0, :, at], halo[phase, 1, 1, :, at]]
            before = None
            for face in range(rows + 1):
                a, b, d, e = full[face : face + 4]
                flux = coef_y[face, :, at] * (7.0 * (b + d) - (a + e))
                if before is not None:
                    u[face - 1, :, at] = z[face - 1, :, at] - (flux - before)
                before = flux

    def low_pass():
        x = jnp.concatenate([u[j] for j in range(rows)], axis=0)
        count = x.shape[0]
        stacked = jnp.concatenate([x[:, q * SEG : (q + 1) * SEG] for q in range(segments)], axis=0)
        part = dot3(stacked, fwd_v[0], fwd_v[1])
        real = jnp.zeros((count, KMAX), F32)
        imag = jnp.zeros((count, KMAX), F32)
        for q in range(segments):
            p = part[q * count : (q + 1) * count, 0:KMAX]
            s = part[q * count : (q + 1) * count, KMAX : 2 * KMAX]
            c_q, s_q = turn_v[2 * q : 2 * q + 1, :], turn_v[2 * q + 1 : 2 * q + 2, :]
            real += c_q * p - s_q * s
            imag += s_q * p + c_q * s
        wave = lax.broadcasted_iota(jnp.int32, (2 * levs, KMAX), 1)
        double = jnp.where(wave == 0, 1.0 / length, 2.0 / length).astype(F32)
        weight = jnp.concatenate(
            [jnp.where(wave <= cut[ilat * rows + j], double, 0.0) for j in range(rows)], axis=0
        )
        real, imag = real * weight, imag * weight
        spread = []
        for q in range(segments):
            c_q, s_q = turn_v[2 * q : 2 * q + 1, :], turn_v[2 * q + 1 : 2 * q + 2, :]
            spread.append(
                jnp.concatenate([real * c_q + imag * s_q, imag * c_q - real * s_q], axis=1)
            )
        back = dot3(jnp.concatenate(spread, axis=0), inv_v[0], inv_v[1])
        for q in range(segments):
            for j in range(rows):
                at = q * count + j * 2 * levs
                u[j, :, q * SEG : (q + 1) * SEG] = back[at : at + 2 * levs]

    exchange_start(0)
    for j in range(rows):
        cx = both(cv[0, j].astype(F32))
        coef_x[j] = (cx + pltpu.roll(cx, length - 1, 1)) * (1.0 / 24.0)
    for j in range(rows):
        z[j] = zonal(u[j], coef_x[j])
    for face in range(1, rows):
        coef_y[face] = (cy_row(face - 1) + cy_row(face)) * (1.0 / 24.0)
    exchange_wait(0)
    for face in (0, rows):
        coef_y[face] = (cy_row(face - 1) + cy_row(face)) * (1.0 / 24.0)
    is_polar = jnp.logical_or(ilat < polar, ilat >= n_lat - polar)
    meridional(0)
    pl.when(is_polar)(low_pass)
    exchange_start(1)
    for j in range(rows):
        z[j] = zonal(u[j], coef_x[j])
    exchange_wait(1)
    meridional(1)
    pl.when(is_polar)(low_pass)

    lane = lax.broadcasted_iota(jnp.int32, (2 * levs, 128), 1)
    low_lane = lane < 64

    @pl.loop(0, n_lev // 2)
    def _(e):
        def tile(j, t):
            return u[j, :, pl.ds(pl.multiple_of(e * width + t * 128, 128), 128)]

        for j in range(rows):
            send[2 * e, j] = tile(j, 0)
            send[2 * e + 1, j] = tile(j, 2)
        for j in range(0, rows, 2):
            one, two = tile(j, 1), tile(j + 1, 1)
            send[2 * e, rows + j // 2] = jnp.where(low_lane, one, pltpu.roll(two, 64, 1))
            send[2 * e + 1, rows + j // 2] = jnp.where(low_lane, pltpu.roll(one, 64, 1), two)

    def offset(step):
        half = lax.div(step + 1, 2)
        return n_lev // 2 + jnp.where(lax.rem(step, 2) == 1, -half, half)

    def column_copy(step):
        other = lax.rem(ilev + offset(step), n_lev)
        return pltpu.make_async_remote_copy(
            src_ref=send.at[other], dst_ref=recv.at[ilev],
            send_sem=a2a_send.at[step], recv_sem=a2a_recv.at[step],
            device_id={"lev": other}, device_id_type=MESH,
        )

    @pl.loop(0, n_lev - 1)
    def _(step):
        column_copy(step).start()

    recv[ilev] = send[ilev]

    count = n_lev * levs
    depth = n_lev * 2 * levs
    source = lax.broadcasted_iota(jnp.int32, (count, depth), 1)
    target = lax.broadcasted_iota(jnp.int32, (count, depth), 0)
    level = lax.div(source, 2 * levs) * levs + lax.rem(source, levs)
    is_heat = lax.rem(source, 2 * levs) >= levs
    pick = (level == target).astype(F32)
    scale = count**-0.5
    deeper = jnp.where(level > target, scale, jnp.where(level == target, 0.5 * scale, 0.0))
    w = wv[...]
    w_high = w.astype(BF16)
    rest = w - w_high.astype(F32)
    w_mid = rest.astype(BF16)
    one_hot = pick.astype(BF16)
    wide_high = jnp.dot(w_high, one_hot, preferred_element_type=F32)
    wide_low = jnp.dot(w_mid, one_hot, preferred_element_type=F32)
    zero = jnp.zeros_like(wide_high)
    map_high = jnp.concatenate(
        [
            jnp.where(is_heat, zero, wide_high),
            jnp.where(is_heat, wide_high, zero),
            jnp.where(is_heat, deeper, zero),
        ],
        axis=0,
    ).astype(BF16)
    map_low = jnp.concatenate(
        [jnp.where(is_heat, zero, wide_low), jnp.where(is_heat, wide_low, zero), zero], axis=0
    ).astype(BF16)

    @pl.loop(0, n_lev - 1)
    def _(step):
        column_copy(step).wait()

    tiles = rows + rows // 2
    x = jnp.concatenate([recv[:, a].reshape(depth, 128) for a in range(tiles)], axis=1)
    x_high, x_low = halves(x)
    y = jnp.dot(map_high, x_high, preferred_element_type=F32)
    y += jnp.dot(map_high, x_low, preferred_element_type=F32)
    y += jnp.dot(map_low, x_high, preferred_element_type=F32)

    low_out = lax.broadcasted_iota(jnp.int32, (count, 128), 1) < 64

    def put(j, f, first, second):
        if f < 2:
            out[f, j, :, 0:128] = first
            out[f, j, :, 128:192] = second[:, 0:64]
        else:
            geo[j, :, 0:128] = first
            geo[j, :, 128:192] = second[:, 0:64]

    @pl.when(parity == 0)
    def _():
        for j in range(rows):
            for f in range(3):
                main = y[f * count : (f + 1) * count, j * 128 : (j + 1) * 128]
                at = (rows + j // 2) * 128
                side = y[f * count : (f + 1) * count, at : at + 128]
                if j % 2 == 1:
                    side = pltpu.roll(side, 64, 1)
                if f == 2:
                    main = main + surf[j : j + 1, 0:128]
                    side = side + surf[j : j + 1, 128:256]
                put(j, f, main, side)

    @pl.when(parity == 1)
    def _():
        for j in range(rows):
            for f in range(3):
                main = y[f * count : (f + 1) * count, j * 128 : (j + 1) * 128]
                at = (rows + j // 2) * 128
                side = y[f * count : (f + 1) * count, at : at + 128]
                if f == 2:
                    main = main + surf[j : j + 1, 256:384]
                    ground = surf[j : j + 1, 128:256]
                    side = side + (pltpu.roll(ground, 64, 1) if j % 2 == 0 else ground)
                if j % 2 == 1:
                    side = pltpu.roll(side, 64, 1)
                main = pltpu.roll(main, 64, 1)
                put(j, f, jnp.where(low_out, side, main), main)


def solution(mesh):
    n_lat, n_lev = mesh.shape["lat"], mesh.shape["lev"]

    def shards(fields, courant, cutoffs, surface, weights):
        _, rows, levs, length = fields.shape
        fwd, inv, turn = fourier_tables(length)
        count = weights.shape[0]
        tiles = rows + rows // 2
        any_spec = pl.BlockSpec(memory_space=pl.ANY)
        vmem_spec = pl.BlockSpec(memory_space=pltpu.VMEM)
        dma = pltpu.SemaphoreType.DMA
        return pl.pallas_call(
            functools.partial(kernel, n_lat, n_lev, 16 // rows),
            out_shape=(
                jax.ShapeDtypeStruct((2, rows, count, length // n_lev), F32),
                jax.ShapeDtypeStruct((rows, count, length // n_lev), F32),
            ),
            in_specs=[any_spec] * 8,
            out_specs=(vmem_spec, vmem_spec),
            scratch_shapes=[
                pltpu.VMEM(courant.shape, BF16),
                pltpu.SMEM(cutoffs.shape, jnp.int32),
                pltpu.VMEM((rows, 384), F32),
                pltpu.VMEM(weights.shape, F32),
                pltpu.VMEM(fwd.shape, BF16),
                pltpu.VMEM(inv.shape, BF16),
                pltpu.VMEM(turn.shape, F32),
                pltpu.VMEM((rows, 2 * levs, length), F32),
                pltpu.VMEM((rows, 2 * levs, length), F32),
                pltpu.VMEM((rows, 2 * levs, length), F32),
                pltpu.VMEM((rows + 1, 2 * levs, length), F32),
                pltpu.VMEM((2, 2, 2, 2 * levs, length), F32),
                pltpu.VMEM((2, levs, length), BF16),
                pltpu.VMEM((n_lev, tiles, 2 * levs, 128), F32),
                pltpu.VMEM((n_lev, tiles, 2 * levs, 128), F32),
                dma((9,)),
                dma((2, 2)),
                dma((2, 2)),
                dma((2,)),
                dma((2,)),
                dma((n_lev - 1,)),
                dma((n_lev - 1,)),
            ],
            compiler_params=pltpu.CompilerParams(collective_id=0, has_side_effects=True),
        )(fields, courant, cutoffs, surface, weights, fwd, inv, turn)

    return jax.shard_map(
        shards,
        mesh=mesh,
        in_specs=(
            P(None, "lat", "lev", None),
            P(None, "lat", "lev", None),
            P(),
            P("lat", None),
            P(),
        ),
        out_specs=(P(None, "lat", None, "lev"), P("lat", None, "lev")),
        check_vma=False,
    )
```

time: 199 us -> 42.2 us (0.21)
  the two profiles are of different devices: /device:TPU:1 before, /device:TPU:7 now
where the time goes in v1:
time: 42.2 us; the launch traced here: 42 us
  Pallas kernels  38.7 us (92%)
  local copies, waits for them, and re-layouts  2.62 us (6%)
  between operations  0.65 us (2%)
    pallas_call x1, Pallas kernels, shards(): pl.pallas_call(functools.partial(kernel, n_lat, n_lev, 16 // rows), out_s...  38.7 us
    unnamed x4, local copies, waits for them, and re-layouts  2.62 us

profile of v1, /device:TPU:7, one launch (start us, length us, event | category | flops | bytes accessed | tf_op | source)
XLA Modules:
  0.0 42.0 jit_solution(1437644190650340738)
XLA Ops:
  0.6 38.7 %shard_map.95 = (f32[2,4,64,192]{3,2,1,0:T(8,128)}, f32[4,64,192]{2,1,0:T(8,128)}) custom-call(f32[2,4,4,3072]{3,2,1,0:T(4,128)} %fields.1, bf16[2,4,4,3072]{3,2,1,0:T(4,128)(2,1)} %courant.1, s32[128]{0:T(128)} %cutoffs.1, f32[4,3072]{1,0:T(4,128)} %surface.1, f32[64,64]{1,0:T(8,128)} %weights.1, bf16[2,256,256]{2,1,0:T(8,128)(2,1)} %constant.6.clone.fwd, ...), custom_call_target="tpu_custom_call" | custom-call | tf_op jit(solution)/shard_map/pallas_call | solution.py:385
  39.4 0.0 copy-start
  39.4 1.9 %copy.12 = f32[2,4,64,192]{3,2,1,0:T(8,128)} copy(f32[2,4,64,192]{3,2,1,0:T(8,128)} %get-tuple-element.4) | data formatting | bytes 786432
  41.3 0.0 copy-done
  41.3 0.7 %copy.13 = f32[4,64,192]{2,1,0:T(8,128)} copy(f32[4,64,192]{2,1,0:T(8,128)S(1)} %copy-done) | data formatting | bytes 393216
Async XLA Ops:
  39.4 1.9 %copy-start = (f32[4,64,192]{2,1,0:T(8,128)S(1)}, f32[4,64,192]{2,1,0:T(8,128)}, u32[]{:S(2)}) copy-start(f32[4,64,192]{2,1,0:T(8,128)} %get-tuple-element.5) | copy-start | bytes 589828

commit v2 on v1

v2 whole, which is shorter than its diff:
```python
import functools

import jax
import jax.numpy as jnp
import numpy as np
from jax import lax
from jax.experimental import pallas as pl
from jax.experimental.pallas import tpu as pltpu
from jax.sharding import PartitionSpec as P

MESH = pl.DeviceIdType.MESH
KMAX = 128
SEG = 256
CODE_MAX = 32767.0
STEPS = 256.0
ROUNDER = 1.5 * 2.0**23
F32 = jnp.float32
BF16 = jnp.bfloat16


def split_bf16(table):
    high = table.astype(np.float32).astype(jnp.bfloat16)
    low = (table - high.astype(np.float64)).astype(np.float32).astype(jnp.bfloat16)
    return np.stack([high, low])


def fourier_tables(length):
    waves = np.arange(KMAX)
    phase = (np.arange(SEG)[:, None] * waves[None, :]) % length
    angle = phase * (2.0 * np.pi / length)
    inner = np.concatenate([np.cos(angle), np.sin(angle)], axis=1)
    segments = length // SEG
    outer = (np.arange(segments)[:, None] * waves[None, :]) % segments
    outer = outer * (2.0 * np.pi / segments)
    turn = np.stack([np.cos(outer), np.sin(outer)], axis=1).astype(np.float32)
    return split_bf16(inner), split_bf16(inner.T), turn.reshape(2 * segments, KMAX)


def halves(x):
    high = x.astype(BF16)
    return high, (x - high.astype(F32)).astype(BF16)


def dot3(x, high, low):
    x_high, x_low = halves(x)
    out = jnp.dot(x_high, high, preferred_element_type=F32)
    out += jnp.dot(x_low, high, preferred_element_type=F32)
    return out + jnp.dot(x_high, low, preferred_element_type=F32)


def zonal(u, coef):
    length = u.shape[-1]
    pair = u + pltpu.roll(u, length - 1, 1)
    face = 8.0 * pair - (pltpu.roll(pair, 1, 1) + pltpu.roll(pair, length - 1, 1))
    flux = coef * face
    return u - (flux - pltpu.roll(flux, 1, 1))


def transport(
    n_lat, n_lev, polar,
    fields, courant, cutoffs, surface, weights, fwd, inv, turn,
    recv, maps, surf,
    cv, cut, wv, fwd_v, inv_v, turn_v,
    u, z, coef_x, coef_y, halo, halo_far, far_stage, cy_halo, send,
    in_sem, near_send, near_recv, far_send, far_recv, cy_send, cy_recv, a2a_send, a2a_recv,
    ring_one, ring_two,
):
    ilat, ilev = lax.axis_index("lat"), lax.axis_index("lev")
    rows, length = u.shape[0], u.shape[2]
    levs = u.shape[1] // 2
    segments = length // SEG
    n_y = n_lev // 2
    y, parity = lax.div(ilev, 2), lax.rem(ilev, 2)
    width = 3 * 128

    loads = [
        pltpu.make_async_copy(fields.at[0], u.at[:, 0:levs, :], in_sem.at[0]),
        pltpu.make_async_copy(fields.at[1], u.at[:, levs : 2 * levs, :], in_sem.at[1]),
        pltpu.make_async_copy(courant, cv, in_sem.at[2]),
        pltpu.make_async_copy(weights, wv, in_sem.at[5]),
        pltpu.make_async_copy(cutoffs, cut, in_sem.at[3]),
        pltpu.make_async_copy(
            surface.at[:, pl.ds(pl.multiple_of(y * width, 128), width)], surf, in_sem.at[4]
        ),
        pltpu.make_async_copy(fwd, fwd_v, in_sem.at[6]),
        pltpu.make_async_copy(inv, inv_v, in_sem.at[7]),
        pltpu.make_async_copy(turn, turn_v, in_sem.at[8]),
    ]

    has_minus, has_plus = ilat > 0, ilat < n_lat - 1
    barrier = pltpu.get_barrier_semaphore()

    def tell(sem, **where):
        pl.semaphore_signal(sem, inc=1, device_id=where, device_id_type=MESH)

    def level(step, core):
        return lax.rem(y + step + n_y, n_y) * 2 + core

    @pl.when(has_minus)
    def _():
        tell(barrier, lat=ilat - 1)

    @pl.when(has_plus)
    def _():
        tell(barrier, lat=ilat + 1)

    for core in range(2):
        tell(barrier, lev=level(1, core))
        tell(barrier, lev=level(-1, core))
    tell(barrier, lev=level(0, 1 - parity))

    for load in loads:
        load.start()

    neighbours = has_minus.astype(jnp.int32) + has_plus.astype(jnp.int32)
    pl.semaphore_wait(barrier, 5 + neighbours)

    def near_copy(phase, side, field):
        row = (rows - 1, 0)[side]
        half = slice(field * levs, (field + 1) * levs)
        source = fields.at[field, row] if phase == 0 else u.at[row, half, :]
        return pltpu.make_async_remote_copy(
            src_ref=source, dst_ref=halo.at[phase, side, half, :],
            send_sem=near_send.at[phase, side, field], recv_sem=near_recv.at[phase, side, field],
            device_id={"lat": ilat + (1, -1)[side]}, device_id_type=MESH,
        )

    def far_copy(phase, side):
        return pltpu.make_async_remote_copy(
            src_ref=far_stage.at[phase, side], dst_ref=halo_far.at[phase, side],
            send_sem=far_send.at[phase, side], recv_sem=far_recv.at[phase, side],
            device_id={"lat": ilat + (1, -1)[side]}, device_id_type=MESH,
        )

    def cy_copy(side):
        return pltpu.make_async_remote_copy(
            src_ref=courant.at[1, (rows - 1, 0)[side]], dst_ref=cy_halo.at[side],
            send_sem=cy_send.at[side], recv_sem=cy_recv.at[side],
            device_id={"lat": ilat + (1, -1)[side]}, device_id_type=MESH,
        )

    there = (has_plus, has_minus)

    def near_start(phase):
        for side in range(2):

            @pl.when(there[side])
            def _():
                near_copy(phase, side, 0).start()
                near_copy(phase, side, 1).start()
                if phase == 0:
                    cy_copy(side).start()

            @pl.when(jnp.logical_not(there[1 - side]))
            def _():
                halo[phase, side] = jnp.zeros(halo.shape[2:], F32)
                halo_far[phase, side] = jnp.zeros(halo_far.shape[2:], BF16)
                if phase == 0:
                    cy_halo[side] = jnp.zeros(cy_halo.shape[1:], BF16)

    def far_start(phase):
        for side in range(2):
            far_stage[phase, side] = u[(rows - 2, 1)[side]].astype(BF16)

            @pl.when(there[side])
            def _():
                far_copy(phase, side).start()

    def exchange_wait(phase):
        for side in range(2):

            @pl.when(there[1 - side])
            def _():
                near_copy(phase, side, 0).wait_recv()
                near_copy(phase, side, 1).wait_recv()
                far_copy(phase, side).wait_recv()
                if phase == 0:
                    cy_copy(side).wait_recv()

            @pl.when(there[side])
            def _():
                near_copy(phase, side, 0).wait_send()
                near_copy(phase, side, 1).wait_send()
                far_copy(phase, side).wait_send()
                if phase == 0:
                    cy_copy(side).wait_send()

    def both(x):
        return jnp.concatenate([x, x], axis=0)

    def cy_row(j):
        if j < 0:
            return both(cy_halo[0].astype(F32))
        if j >= rows:
            return both(cy_halo[1].astype(F32))
        return both(cv[1, j].astype(F32))

    def meridional(phase, start, piece):
        at = pl.ds(pl.multiple_of(start, 128), piece)
        full = [halo_far[phase, 0, :, at].astype(F32), halo[phase, 0, :, at]]
        full += [u[j, :, at] for j in range(rows)]
        full += [halo[phase, 1, :, at], halo_far[phase, 1, :, at].astype(F32)]
        before = None
        for face in range(rows + 1):
            a, b, d, e = full[face : face + 4]
            flux = coef_y[face, :, at] * (7.0 * (b + d) - (a + e))
            if before is not None:
                u[face - 1, :, at] = z[face - 1, :, at] - (flux - before)
            before = flux

    def low_pass():
        x = jnp.concatenate([u[j] for j in range(rows)], axis=0)
        count = x.shape[0]
        stacked = jnp.concatenate([x[:, q * SEG : (q + 1) * SEG] for q in range(segments)], axis=0)
        part = dot3(stacked, fwd_v[0], fwd_v[1])
        real = jnp.zeros((count, KMAX), F32)
        imag = jnp.zeros((count, KMAX), F32)
        for q in range(segments):
            p = part[q * count : (q + 1) * count, 0:KMAX]
            s = part[q * count : (q + 1) * count, KMAX : 2 * KMAX]
            c_q, s_q = turn_v[2 * q : 2 * q + 1, :], turn_v[2 * q + 1 : 2 * q + 2, :]
            real += c_q * p - s_q * s
            imag += s_q * p + c_q * s
        wave = lax.broadcasted_iota(jnp.int32, (2 * levs, KMAX), 1)
        double = jnp.where(wave == 0, 1.0 / length, 2.0 / length).astype(F32)
        weight = jnp.concatenate(
            [jnp.where(wave <= cut[ilat * rows + j], double, 0.0) for j in range(rows)], axis=0
        )
        real, imag = real * weight, imag * weight
        spread = []
        for q in range(segments):
            c_q, s_q = turn_v[2 * q : 2 * q + 1, :], turn_v[2 * q + 1 : 2 * q + 2, :]
            spread.append(
                jnp.concatenate([real * c_q + imag * s_q, imag * c_q - real * s_q], axis=1)
            )
        back = dot3(jnp.concatenate(spread, axis=0), inv_v[0], inv_v[1])
        for q in range(segments):
            for j in range(rows):
                at = q * count + j * 2 * levs
                u[j, :, q * SEG : (q + 1) * SEG] = back[at : at + 2 * levs]

    tiles = rows + rows // 2
    low_lane = lax.broadcasted_iota(jnp.int32, (2 * levs, 128), 1) < 64

    def encode(slot, parts):
        most = jnp.abs(parts[0])
        for part in parts[1:]:
            most = jnp.maximum(most, jnp.abs(part))
        power = jnp.ceil(jnp.log2(jnp.maximum(most, 1e-30)) * STEPS + 0.01)
        to_code = jnp.exp2(power * (-1.0 / STEPS)) * CODE_MAX
        for a, part in enumerate(parts):
            code = jnp.clip((part * to_code + ROUNDER) - ROUNDER, -CODE_MAX, CODE_MAX)
            send[slot, a] = code.astype(jnp.int32).astype(jnp.int16)
        send[slot, tiles] = power.astype(jnp.int32).astype(jnp.int16)

    def pack(e):
        def tile(j, t):
            return u[j, :, pl.ds(pl.multiple_of(e * width + t * 128, 128), 128)]

        first = [tile(j, 0) for j in range(rows)]
        second = [tile(j, 2) for j in range(rows)]
        for j in range(0, rows, 2):
            one, two = tile(j, 1), tile(j + 1, 1)
            first.append(jnp.where(low_lane, one, pltpu.roll(two, 64, 1)))
            second.append(jnp.where(low_lane, pltpu.roll(one, 64, 1), two))
        encode(2 * e, first)
        encode(2 * e + 1, second)

    def target(step):
        half = lax.div(step + 1, 2)
        return lax.rem(y + n_y // 2 + jnp.where(lax.rem(step, 2) == 1, -half, half), n_y)

    def column_copy(step, core):
        other = target(step) * 2 + core
        return pltpu.make_async_remote_copy(
            src_ref=send.at[other], dst_ref=recv.at[ilev],
            send_sem=a2a_send.at[step, core], recv_sem=a2a_recv.at[step, parity],
            device_id={"lev": other}, device_id_type=MESH,
        )

    def column_arrival(step, core):
        return pltpu.make_async_remote_copy(
            src_ref=send.at[0], dst_ref=recv.at[ilev],
            send_sem=a2a_send.at[step, core], recv_sem=a2a_recv.at[step, core],
            device_id={"lev": ilev}, device_id_type=MESH,
        )

    def columns(before):
        @pl.loop(0, n_y - 1)
        def _(step):
            e = target(step)
            before(e)
            pack(e)
            column_copy(step, 0).start()
            column_copy(step, 1).start()

        before(y)
        pack(y)
        column_copy(n_y - 1, 1 - parity).start()
        recv[ilev] = send[ilev]

    near_start(0)
    for load in loads[:2]:
        load.wait()
    far_start(0)
    tell(ring_one, lev=level(1, parity))
    tell(ring_one, lev=level(-1, parity))
    for load in loads[2:]:
        load.wait()
    for j in range(rows):
        cx = both(cv[0, j].astype(F32))
        coef_x[j] = (cx + pltpu.roll(cx, length - 1, 1)) * (1.0 / 24.0)
    for j in range(rows):
        z[j] = zonal(u[j], coef_x[j])
    for face in range(1, rows):
        coef_y[face] = (cy_row(face - 1) + cy_row(face)) * (1.0 / 24.0)
    exchange_wait(0)
    for face in (0, rows):
        coef_y[face] = (cy_row(face - 1) + cy_row(face)) * (1.0 / 24.0)
    is_polar = jnp.logical_or(ilat < polar, ilat >= n_lat - polar)

    @pl.loop(0, length // 512)
    def _(c):
        meridional(0, c * 512, 512)

    pl.when(is_polar)(low_pass)
    near_start(1)
    far_start(1)
    pl.semaphore_wait(ring_one, 2)
    tell(ring_two, lev=level(2, parity))
    tell(ring_two, lev=level(-2, parity))
    for j in range(rows):
        z[j] = zonal(u[j], coef_x[j])
    write_maps(n_lev, levs, wv, maps)
    pl.semaphore_wait(ring_two, 2)
    exchange_wait(1)

    @pl.when(is_polar)
    def _():
        @pl.loop(0, length // 512)
        def _(c):
            meridional(1, c * 512, 512)

        low_pass()
        columns(lambda e: None)

    @pl.when(jnp.logical_not(is_polar))
    def _():
        columns(lambda e: meridional(1, e * width, width))

    @pl.loop(0, n_y - 1)
    def _(step):
        for core in range(2):
            column_copy(step, core).wait_send()
            column_arrival(step, core).wait_recv()

    column_copy(n_y - 1, 1 - parity).wait_send()
    column_arrival(n_y - 1, 1 - parity).wait_recv()


def write_maps(n_lev, levs, wv, maps):
    count = n_lev * levs
    depth = n_lev * 2 * levs
    source = lax.broadcasted_iota(jnp.int32, (count, depth), 1)
    goal = lax.broadcasted_iota(jnp.int32, (count, depth), 0)
    level = lax.div(source, 2 * levs) * levs + lax.rem(source, levs)
    is_heat = lax.rem(source, 2 * levs) >= levs
    scale = count**-0.5
    deeper = jnp.where(level > goal, scale, jnp.where(level == goal, 0.5 * scale, 0.0))
    w_high, w_low = halves(wv[...])
    one_hot = (level == goal).astype(F32).astype(BF16)
    for half, w in enumerate((w_high, w_low)):
        wide = jnp.dot(w, one_hot, preferred_element_type=F32)
        maps[half, 0:count, :] = jnp.where(is_heat, 0.0, wide).astype(BF16)
        maps[half, count : 2 * count, :] = jnp.where(is_heat, wide, 0.0).astype(BF16)
    maps[0, 2 * count : 3 * count, :] = jnp.where(is_heat, deeper, 0.0).astype(BF16)
    maps[1, 2 * count : 3 * count, :] = jnp.zeros((count, depth), BF16)


def remap(recv, maps, surf, out, geo, out_v, geo_v, out_sem, geo_sem):
    n_lev, tiles, depth_rows = recv.shape[0], recv.shape[1] - 1, recv.shape[2]
    rows = surf.shape[0]
    count = maps.shape[1] // 3
    depth = n_lev * depth_rows
    parity = lax.rem(lax.axis_index("lev"), 2)
    scale = jnp.exp2(recv[:, tiles].astype(jnp.int32).astype(F32) * (1.0 / STEPS))
    scale = (scale * (1.0 / CODE_MAX)).reshape(depth, 128)
    values = [
        recv[:, a].astype(jnp.int32).astype(F32).reshape(depth, 128) * scale for a in range(tiles)
    ]
    x_high, x_low = halves(jnp.concatenate(values, axis=1))
    y = jnp.dot(maps[0], x_high, preferred_element_type=F32)
    y += jnp.dot(maps[0], x_low, preferred_element_type=F32)
    y += jnp.dot(maps[1], x_high, preferred_element_type=F32)
    low_out = lax.broadcasted_iota(jnp.int32, (count, 128), 1) < 64

    def put(j, f, first, second):
        if f < 2:
            out_v[f, j, :, 0:128] = first
            out_v[f, j, :, 128:192] = second[:, 0:64]
        else:
            geo_v[j, :, 0:128] = first
            geo_v[j, :, 128:192] = second[:, 0:64]

    @pl.when(parity == 0)
    def _():
        for j in range(rows):
            for f in range(3):
                main = y[f * count : (f + 1) * count, j * 128 : (j + 1) * 128]
                at = (rows + j // 2) * 128
                side = y[f * count : (f + 1) * count, at : at + 128]
                if j % 2 == 1:
                    side = pltpu.roll(side, 64, 1)
                if f == 2:
                    main = main + surf[j : j + 1, 0:128]
                    side = side + surf[j : j + 1, 128:256]
                put(j, f, main, side)

    @pl.when(parity == 1)
    def _():
        for j in range(rows):
            for f in range(3):
                main = y[f * count : (f + 1) * count, j * 128 : (j + 1) * 128]
                at = (rows + j // 2) * 128
                side = y[f * count : (f + 1) * count, at : at + 128]
                if f == 2:
                    main = main + surf[j : j + 1, 256:384]
                    ground = surf[j : j + 1, 128:256]
                    side = side + (pltpu.roll(ground, 64, 1) if j % 2 == 0 else ground)
                if j % 2 == 1:
                    side = pltpu.roll(side, 64, 1)
                main = pltpu.roll(main, 64, 1)
                put(j, f, jnp.where(low_out, side, main), main)

    for j in range(rows):
        copies = [pltpu.make_async_copy(out_v.at[f, j], out.at[f, j], out_sem.at[f, j]) for f in range(2)]
        copies.append(pltpu.make_async_copy(geo_v.at[j], geo.at[j], geo_sem.at[j]))
        for copy in copies:
            copy.start()
    for j in range(rows):
        for f in range(2):
            pltpu.make_async_copy(out_v.at[f, j], out.at[f, j], out_sem.at[f, j]).wait()
        pltpu.make_async_copy(geo_v.at[j], geo.at[j], geo_sem.at[j]).wait()


def solution(mesh):
    n_lat, n_lev = mesh.shape["lat"], mesh.shape["lev"]

    def shards(fields, courant, cutoffs, surface, weights):
        _, rows, levs, length = fields.shape
        fwd, inv, turn = fourier_tables(length)
        count = weights.shape[0]
        tiles = rows + rows // 2
        hbm_spec = pl.BlockSpec(memory_space=pltpu.HBM)
        vmem_spec = pl.BlockSpec(memory_space=pltpu.VMEM)
        dma = pltpu.SemaphoreType.DMA
        recv, maps, surf = pl.pallas_call(
            functools.partial(transport, n_lat, n_lev, 16 // rows),
            name="transport",
            out_shape=(
                pltpu.VMEM((n_lev, tiles + 1, 2 * levs, 128), jnp.int16),
                pltpu.VMEM((2, 3 * count, 2 * count), BF16),
                pltpu.VMEM((rows, 384), F32),
            ),
            in_specs=[hbm_spec] * 8,
            out_specs=(vmem_spec,) * 3,
            scratch_shapes=[
                pltpu.VMEM(courant.shape, BF16),
                pltpu.SMEM(cutoffs.shape, jnp.int32),
                pltpu.VMEM(weights.shape, F32),
                pltpu.VMEM(fwd.shape, BF16),
                pltpu.VMEM(inv.shape, BF16),
                pltpu.VMEM(turn.shape, F32),
                pltpu.VMEM((rows, 2 * levs, length), F32),
                pltpu.VMEM((rows, 2 * levs, length), F32),
                pltpu.VMEM((rows, 2 * levs, length), F32),
                pltpu.VMEM((rows + 1, 2 * levs, length), F32),
                pltpu.VMEM((2, 2, 2 * levs, length), F32),
                pltpu.VMEM((2, 2, 2 * levs, length), BF16),
                pltpu.VMEM((2, 2, 2 * levs, length), BF16),
                pltpu.VMEM((2, levs, length), BF16),
                pltpu.VMEM((n_lev, tiles + 1, 2 * levs, 128), jnp.int16),
                dma((9,)),
                dma((2, 2, 2)),
                dma((2, 2, 2)),
                dma((2, 2)),
                dma((2, 2)),
                dma((2,)),
                dma((2,)),
                dma((n_lev // 2, 2)),
                dma((n_lev // 2, 2)),
                pltpu.SemaphoreType.REGULAR,
                pltpu.SemaphoreType.REGULAR,
            ],
            compiler_params=pltpu.CompilerParams(
                collective_id=0, has_side_effects=True
            ),
        )(fields, courant, cutoffs, surface, weights, fwd, inv, turn)
        columns = length // n_lev
        return pl.pallas_call(
            remap,
            name="remap",
            out_shape=(
                jax.ShapeDtypeStruct((2, rows, count, columns), F32),
                jax.ShapeDtypeStruct((rows, count, columns), F32),
            ),
            in_specs=[vmem_spec] * 3,
            out_specs=(hbm_spec, hbm_spec),
            scratch_shapes=[
                pltpu.VMEM((2, rows, count, columns), F32),
                pltpu.VMEM((rows, count, columns), F32),
                dma((2, rows)),
                dma((rows,)),
            ],
            compiler_params=pltpu.CompilerParams(vmem_limit_bytes=24 << 20),
        )(recv, maps, surf)

    return jax.shard_map(
        shards,
        mesh=mesh,
        in_specs=(
            P(None, "lat", "lev", None),
            P(None, "lat", "lev", None),
            P(),
            P("lat", None),
            P(),
        ),
        out_specs=(P(None, "lat", None, "lev"), P("lat", None, "lev")),
        check_vma=False,
    )
```

time: 42.2 us -> 33.2 us (0.79)
  Pallas kernels: 38.7 us -> 32.4 us
  local copies, waits for them, and re-layouts: 2.62 us -> 0 us
    pallas_call x1 -> x2, Pallas kernels: 38.7 us -> 32.4 us  [the longest x1 30.8 us: shards(): pl.pallas_call(functools.partial(transport, n_lat, n_lev, 16 // rows), na...]
    unnamed x4 -> x0, local copies, waits for them, and re-layouts: 2.62 us -> none
where the time goes in v2:
time: 33.2 us; the launch traced here: 33 us
  Pallas kernels  32.4 us (98%)
  between operations  0.64 us (2%)
    pallas_call x1, Pallas kernels, shards(): pl.pallas_call(functools.partial(transport, n_lat, n_lev, 16 // rows), na...  30.8 us
    pallas_call x1, Pallas kernels, shards(): pl.pallas_call(remap, name='remap', out_shape=(jax.ShapeDtypeStruct((2, r...  1.62 us

profile of v2, /device:TPU:7, one launch (start us, length us, event | category | flops | bytes accessed | tf_op | source)
XLA Modules:
  0.0 33.0 jit_solution(16352046976601109165)
XLA Ops:
  0.6 30.8 %transport.1 = (s16[16,7,8,128]{3,2,1,0:T(8,128)(2,1)S(1)}, bf16[2,192,128]{2,1,0:T(8,128)(2,1)S(1)}, f32[4,384]{1,0:T(4,128)S(1)}) custom-call(f32[2,4,4,3072]{3,2,1,0:T(4,128)} %fields.1, bf16[2,4,4,3072]{3,2,1,0:T(4,128)(2,1)} %courant.1, s32[128]{0:T(128)} %cutoffs.1, f32[4,3072]{1,0:T(4,128)} %surface.1, f32[64,64]{1,0:T(8,128)} %weights.1, ...), custom_call_target="tpu_custom_call" | custom-call | tf_op jit(solution)/shard_map/transport/pallas_call | solution.py:457
  31.4 1.6 %remap.1 = (f32[2,4,64,192]{3,2,1,0:T(8,128)}, f32[4,64,192]{2,1,0:T(8,128)}) custom-call(s16[16,7,8,128]{3,2,1,0:T(8,128)(2,1)S(1)} %get-tuple-element.5.recv, bf16[2,192,128]{2,1,0:T(8,128)(2,1)S(1)} %get-tuple-element.6.maps, f32[4,384]{1,0:T(4,128)S(1)} %get-tuple-element.7.surf), custom_call_target="tpu_custom_call" | custom-call | tf_op jit(solution)/shard_map/remap/pallas_call | solution.py:500

commit v3 on v2

--- a/solution.py
+++ b/solution.py
@@ -61,8 +61,8 @@
     fields, courant, cutoffs, surface, weights, fwd, inv, turn,
     recv, maps, surf,
     cv, cut, wv, fwd_v, inv_v, turn_v,
-    u, z, coef_x, coef_y, halo, halo_far, far_stage, cy_halo, send,
-    in_sem, near_send, near_recv, far_send, far_recv, cy_send, cy_recv, a2a_send, a2a_recv,
+    u, v, z, coef_x, coef_y, near, far, far_stage, cx_halo, cy_halo, send,
+    in_sem, halo_send, halo_recv, a2a_send, a2a_recv,
     ring_one, ring_two,
 ):
     ilat, ilev = lax.axis_index("lat"), lax.axis_index("lev")
@@ -109,107 +109,138 @@
         tell(barrier, lev=level(-1, core))
     tell(barrier, lev=level(0, 1 - parity))
 
-    for load in loads:
+    for load in loads[:3]:
         load.start()
 
     neighbours = has_minus.astype(jnp.int32) + has_plus.astype(jnp.int32)
     pl.semaphore_wait(barrier, 5 + neighbours)
 
-    def near_copy(phase, side, field):
+    def halo_copies(side):
         row = (rows - 1, 0)[side]
-        half = slice(field * levs, (field + 1) * levs)
-        source = fields.at[field, row] if phase == 0 else u.at[row, half, :]
-        return pltpu.make_async_remote_copy(
-            src_ref=source, dst_ref=halo.at[phase, side, half, :],
-            send_sem=near_send.at[phase, side, field], recv_sem=near_recv.at[phase, side, field],
-            device_id={"lat": ilat + (1, -1)[side]}, device_id_type=MESH,
-        )
-
-    def far_copy(phase, side):
-        return pltpu.make_async_remote_copy(
-            src_ref=far_stage.at[phase, side], dst_ref=halo_far.at[phase, side],
-            send_sem=far_send.at[phase, side], recv_sem=far_recv.at[phase, side],
-            device_id={"lat": ilat + (1, -1)[side]}, device_id_type=MESH,
-        )
-
-    def cy_copy(side):
-        return pltpu.make_async_remote_copy(
-            src_ref=courant.at[1, (rows - 1, 0)[side]], dst_ref=cy_halo.at[side],
-            send_sem=cy_send.at[side], recv_sem=cy_recv.at[side],
-            device_id={"lat": ilat + (1, -1)[side]}, device_id_type=MESH,
-        )
+        pieces = [
+            (fields.at[0, row], near.at[side, 0:levs, :]),
+            (fields.at[1, row], near.at[side, levs : 2 * levs, :]),
+            (courant.at[1, pl.ds((1, 0)[side], 3)], cy_halo.at[side]),
+            (courant.at[0, pl.ds((2, 0)[side], 2)], cx_halo.at[side]),
+            (far_stage.at[pl.ds((0, 1)[side], 3)], far.at[side]),
+        ]
+        return [
+            pltpu.make_async_remote_copy(
+                src_ref=source, dst_ref=goal,
+                send_sem=halo_send.at[side, n], recv_sem=halo_recv.at[side, n],
+                device_id={"lat": ilat + (1, -1)[side]}, device_id_type=MESH,
+            )
+            for n, (source, goal) in enumerate(pieces)
+        ]
 
     there = (has_plus, has_minus)
 
-    def near_start(phase):
-        for side in range(2):
+    def halo_start(first, last):
+        for side in (0, 1):
 
             @pl.when(there[side])
             def _():
-                near_copy(phase, side, 0).start()
-                near_copy(phase, side, 1).start()
-                if phase == 0:
-                    cy_copy(side).start()
-
-            @pl.when(jnp.logical_not(there[1 - side]))
-            def _():
-                halo[phase, side] = jnp.zeros(halo.shape[2:], F32)
-                halo_far[phase, side] = jnp.zeros(halo_far.shape[2:], BF16)
-                if phase == 0:
-                    cy_halo[side] = jnp.zeros(cy_halo.shape[1:], BF16)
-
-    def far_start(phase):
-        for side in range(2):
-            far_stage[phase, side] = u[(rows - 2, 1)[side]].astype(BF16)
-
-            @pl.when(there[side])
-            def _():
-                far_copy(phase, side).start()
-
-    def exchange_wait(phase):
-        for side in range(2):
-
-            @pl.when(there[1 - side])
-            def _():
-                near_copy(phase, side, 0).wait_recv()
-                near_copy(phase, side, 1).wait_recv()
-                far_copy(phase, side).wait_recv()
-                if phase == 0:
-                    cy_copy(side).wait_recv()
-
-            @pl.when(there[side])
-            def _():
-                near_copy(phase, side, 0).wait_send()
-                near_copy(phase, side, 1).wait_send()
-                far_copy(phase, side).wait_send()
-                if phase == 0:
-                    cy_copy(side).wait_send()
+                for copy in halo_copies(side)[first:last]:
+                    copy.start()
+
+    def halo_wait(side):
+        @pl.when(there[1 - side])
+        def _():
+            for copy in halo_copies(side):
+                copy.wait_recv()
+
+        @pl.when(jnp.logical_not(there[1 - side]))
+        def _():
+            near[side] = jnp.zeros(near.shape[1:], F32)
+            far[side] = jnp.zeros(far.shape[1:], BF16)
+            cx_halo[side] = jnp.zeros(cx_halo.shape[1:], BF16)
+            cy_halo[side] = jnp.zeros(cy_halo.shape[1:], BF16)
 
     def both(x):
         return jnp.concatenate([x, x], axis=0)
 
-    def cy_row(j):
-        if j < 0:
-            return both(cy_halo[0].astype(F32))
-        if j >= rows:
-            return both(cy_halo[1].astype(F32))
-        return both(cv[1, j].astype(F32))
-
-    def meridional(phase, start, piece):
+    def cy_row(r):
+        if r < 0:
+            return both(cy_halo[0, r + 3].astype(F32))
+        if r >= rows:
+            return both(cy_halo[1, r - rows].astype(F32))
+        return both(cv[1, r].astype(F32))
+
+    def cx_row(r):
+        if r < 0:
+            return both(cx_halo[0, r + 2].astype(F32))
+        if r >= rows:
+            return both(cx_halo[1, r - rows].astype(F32))
+        return both(cv[0, r].astype(F32))
+
+    def u_row(r, at=slice(None)):
+        if r == -1:
+            return near[0, :, at]
+        if r < 0:
+            return far[0, r + 4, :, at].astype(F32)
+        if r == rows:
+            return near[1, :, at]
+        if r > rows:
+            return far[1, r - rows - 1, :, at].astype(F32)
+        return u[r, :, at]
+
+    def v_row(r, at=slice(None)):
+        return v[r + 2, :, at]
+
+    def set_coef_x(r):
+        cx = cx_row(r)
+        coef_x[r + 2] = (cx + pltpu.roll(cx, length - 1, 1)) * (1.0 / 24.0)
+
+    def set_coef_y(r):
+        coef_y[r + 3] = (cy_row(r) + cy_row(r + 1)) * (1.0 / 24.0)
+
+    def meridional(source, goal, shift, first, count, start, piece):
         at = pl.ds(pl.multiple_of(start, 128), piece)
-        full = [halo_far[phase, 0, :, at].astype(F32), halo[phase, 0, :, at]]
-        full += [u[j, :, at] for j in range(rows)]
-        full += [halo[phase, 1, :, at], halo_far[phase, 1, :, at].astype(F32)]
+        full = [source(r, at) for r in range(first - 2, first + count + 2)]
         before = None
-        for face in range(rows + 1):
-            a, b, d, e = full[face : face + 4]
-            flux = coef_y[face, :, at] * (7.0 * (b + d) - (a + e))
+        for n in range(count + 1):
+            a, b, d, e = full[n : n + 4]
+            r = first + n - 1
+            flux = coef_y[r + 3, :, at] * (7.0 * (b + d) - (a + e))
             if before is not None:
-                u[face - 1, :, at] = z[face - 1, :, at] - (flux - before)
+                goal[r + shift, :, at] = z[r + 2, :, at] - (flux - before)
             before = flux
 
-    def low_pass():
-        x = jnp.concatenate([u[j] for j in range(rows)], axis=0)
+    def first_substep(side):
+        half = rows // 2
+        if side == 0:
+            group, outer, faces, other = -2, (-2, -1), (-3, -2, -1), ilat - 1
+        else:
+            group, outer, other = half, (rows, rows + 1), ilat + 1
+            faces = (rows - 1, rows, rows + 1)
+        for r in faces:
+            set_coef_y(r)
+        for r in outer:
+            set_coef_x(r)
+            z[r + 2] = zonal(u_row(r), coef_x[r + 2])
+
+        @pl.loop(0, length // 512)
+        def _(c):
+            meridional(u_row, v, 2, group, rows, c * 512, 512)
+
+        @pl.when(jnp.logical_not(there[1 - side]))
+        def _():
+            for r in outer:
+                v[r + 2] = jnp.zeros(v.shape[1:], F32)
+
+        def band_is_polar(band):
+            return jnp.logical_or(band < polar, band >= n_lat - polar)
+
+        @pl.when(jnp.logical_or(band_is_polar(ilat), band_is_polar(other)))
+        def _():
+            low_pass(v, group + 2, group)
+
+        for r in range(max(group, 0), min(group + rows, rows)):
+            z[r + 2] = zonal(v_row(r), coef_x[r + 2])
+
+    def low_pass(ref, base, first):
+        x = jnp.concatenate([ref[base + j] for j in range(rows)], axis=0)
+        cuts = [cut[jnp.clip(ilat * rows + first + j, 0, n_lat * rows - 1)] for j in range(rows)]
         count = x.shape[0]
         stacked = jnp.concatenate([x[:, q * SEG : (q + 1) * SEG] for q in range(segments)], axis=0)
         part = dot3(stacked, fwd_v[0], fwd_v[1])
@@ -224,7 +255,7 @@
         wave = lax.broadcasted_iota(jnp.int32, (2 * levs, KMAX), 1)
         double = jnp.where(wave == 0, 1.0 / length, 2.0 / length).astype(F32)
         weight = jnp.concatenate(
-            [jnp.where(wave <= cut[ilat * rows + j], double, 0.0) for j in range(rows)], axis=0
+            [jnp.where(wave <= cuts[j], double, 0.0) for j in range(rows)], axis=0
         )
         real, imag = real * weight, imag * weight
         spread = []
@@ -237,7 +268,10 @@
         for q in range(segments):
             for j in range(rows):
                 at = q * count + j * 2 * levs
-                u[j, :, q * SEG : (q + 1) * SEG] = back[at : at + 2 * levs]
+                piece = slice(q * SEG, (q + 1) * SEG)
+                ref[base + j, :, piece] = jnp.where(
+                    cuts[j] < length // 2, back[at : at + 2 * levs], ref[base + j, :, piece]
+                )
 
     tiles = rows + rows // 2
     low_lane = lax.broadcasted_iota(jnp.int32, (2 * levs, 128), 1) < 64
@@ -299,54 +333,53 @@
         column_copy(n_y - 1, 1 - parity).start()
         recv[ilev] = send[ilev]
 
-    near_start(0)
+    halo_start(0, 4)
+    for load in loads[3:]:
+        load.start()
     for load in loads[:2]:
         load.wait()
-    far_start(0)
+    for r in range(rows):
+        far_stage[r] = u[r].astype(BF16)
+    halo_start(4, 5)
     tell(ring_one, lev=level(1, parity))
     tell(ring_one, lev=level(-1, parity))
     for load in loads[2:]:
         load.wait()
-    for j in range(rows):
-        cx = both(cv[0, j].astype(F32))
-        coef_x[j] = (cx + pltpu.roll(cx, length - 1, 1)) * (1.0 / 24.0)
-    for j in range(rows):
-        z[j] = zonal(u[j], coef_x[j])
-    for face in range(1, rows):
-        coef_y[face] = (cy_row(face - 1) + cy_row(face)) * (1.0 / 24.0)
-    exchange_wait(0)
-    for face in (0, rows):
-        coef_y[face] = (cy_row(face - 1) + cy_row(face)) * (1.0 / 24.0)
-    is_polar = jnp.logical_or(ilat < polar, ilat >= n_lat - polar)
-
-    @pl.loop(0, length // 512)
-    def _(c):
-        meridional(0, c * 512, 512)
-
-    pl.when(is_polar)(low_pass)
-    near_start(1)
-    far_start(1)
+    for r in range(rows):
+        set_coef_x(r)
+        z[r + 2] = zonal(u[r], coef_x[r + 2])
+    for r in range(rows - 1):
+        set_coef_y(r)
+    write_maps(n_lev, levs, wv, maps)
+    halo_wait(1)
+    first_substep(1)
     pl.semaphore_wait(ring_one, 2)
     tell(ring_two, lev=level(2, parity))
     tell(ring_two, lev=level(-2, parity))
-    for j in range(rows):
-        z[j] = zonal(u[j], coef_x[j])
-    write_maps(n_lev, levs, wv, maps)
+    halo_wait(0)
+    first_substep(0)
     pl.semaphore_wait(ring_two, 2)
-    exchange_wait(1)
+    is_polar = jnp.logical_or(ilat < polar, ilat >= n_lat - polar)
 
     @pl.when(is_polar)
     def _():
         @pl.loop(0, length // 512)
         def _(c):
-            meridional(1, c * 512, 512)
-
-        low_pass()
+            meridional(v_row, u, 0, 0, rows, c * 512, 512)
+
+        low_pass(u, 0, 0)
         columns(lambda e: None)
 
     @pl.when(jnp.logical_not(is_polar))
     def _():
-        columns(lambda e: meridional(1, e * width, width))
+        columns(lambda e: meridional(v_row, u, 0, 0, rows, e * width, width))
+
+    for side in (0, 1):
+
+        @pl.when(there[side])
+        def _():
+            for copy in halo_copies(side):
+                copy.wait_send()
 
     @pl.loop(0, n_y - 1)
     def _(step):
@@ -472,21 +505,19 @@
                 pltpu.VMEM(inv.shape, BF16),
                 pltpu.VMEM(turn.shape, F32),
                 pltpu.VMEM((rows, 2 * levs, length), F32),
-                pltpu.VMEM((rows, 2 * levs, length), F32),
-                pltpu.VMEM((rows, 2 * levs, length), F32),
-                pltpu.VMEM((rows + 1, 2 * levs, length), F32),
-                pltpu.VMEM((2, 2, 2 * levs, length), F32),
-                pltpu.VMEM((2, 2, 2 * levs, length), BF16),
-                pltpu.VMEM((2, 2, 2 * levs, length), BF16),
-                pltpu.VMEM((2, levs, length), BF16),
+                pltpu.VMEM((rows + 4, 2 * levs, length), F32),
+                pltpu.VMEM((rows + 4, 2 * levs, length), F32),
+                pltpu.VMEM((rows + 4, 2 * levs, length), F32),
+                pltpu.VMEM((rows + 5, 2 * levs, length), F32),
+                pltpu.VMEM((2, 2 * levs, length), F32),
+                pltpu.VMEM((2, 3, 2 * levs, length), BF16),
+                pltpu.VMEM((rows, 2 * levs, length), BF16),
+                pltpu.VMEM((2, 2, levs, length), BF16),
+                pltpu.VMEM((2, 3, levs, length), BF16),
                 pltpu.VMEM((n_lev, tiles + 1, 2 * levs, 128), jnp.int16),
                 dma((9,)),
-                dma((2, 2, 2)),
-                dma((2, 2, 2)),
-                dma((2, 2)),
-                dma((2, 2)),
-                dma((2,)),
-                dma((2,)),
+                dma((2, 5)),
+                dma((2, 5)),
                 dma((n_lev // 2, 2)),
                 dma((n_lev // 2, 2)),
                 pltpu.SemaphoreType.REGULAR,

time: 33.2 us -> 33.7 us (1.015)
  Pallas kernels: 32.4 us -> 32.9 us
    pallas_call x1, Pallas kernels: 30.8 us -> 31.3 us  [shards(): pl.pallas_call(functools.partial(transport, n_lat, n_lev, 16 // rows), na...]
where the time goes in v3:
time: 33.7 us; the launch traced here: 33.6 us
  Pallas kernels  32.9 us (98%)
  between operations  0.64 us (2%)
    pallas_call x1, Pallas kernels, shards(): pl.pallas_call(functools.partial(transport, n_lat, n_lev, 16 // rows), na...  31.3 us
    pallas_call x1, Pallas kernels, shards(): pl.pallas_call(remap, name='remap', out_shape=(jax.ShapeDtypeStruct((2, r...  1.62 us

profile of v3, /device:TPU:7, one launch (start us, length us, event | category | flops | bytes accessed | tf_op | source)
XLA Modules:
  0.0 33.6 jit_solution(2972546478612494475)
XLA Ops:
  0.6 31.3 %transport.1 = (s16[16,7,8,128]{3,2,1,0:T(8,128)(2,1)S(1)}, bf16[2,192,128]{2,1,0:T(8,128)(2,1)S(1)}, f32[4,384]{1,0:T(4,128)S(1)}) custom-call(f32[2,4,4,3072]{3,2,1,0:T(4,128)} %fields.1, bf16[2,4,4,3072]{3,2,1,0:T(4,128)(2,1)} %courant.1, s32[128]{0:T(128)} %cutoffs.1, f32[4,3072]{1,0:T(4,128)} %surface.1, f32[64,64]{1,0:T(8,128)} %weights.1, ...), custom_call_target="tpu_custom_call" | custom-call | tf_op jit(solution)/shard_map/transport/pallas_call | solution.py:490
  31.9 1.6 %remap.1 = (f32[2,4,64,192]{3,2,1,0:T(8,128)}, f32[4,64,192]{2,1,0:T(8,128)}) custom-call(s16[16,7,8,128]{3,2,1,0:T(8,128)(2,1)S(1)} %get-tuple-element.5.recv, bf16[2,192,128]{2,1,0:T(8,128)(2,1)S(1)} %get-tuple-element.6.maps, f32[4,384]{1,0:T(4,128)S(1)} %get-tuple-element.7.surf), custom_call_target="tpu_custom_call" | custom-call | tf_op jit(solution)/shard_map/remap/pallas_call | solution.py:531

commit v4 on v3

--- a/solution.py
+++ b/solution.py
@@ -61,7 +61,7 @@
     fields, courant, cutoffs, surface, weights, fwd, inv, turn,
     recv, maps, surf,
     cv, cut, wv, fwd_v, inv_v, turn_v,
-    u, v, z, coef_x, coef_y, near, far, far_stage, cx_halo, cy_halo, send,
+    u, v, z, coef_x, coef_y, near, far, stage, cy_halo, send,
     in_sem, halo_send, halo_recv, a2a_send, a2a_recv,
     ring_one, ring_two,
 ):
@@ -120,9 +120,9 @@
         pieces = [
             (fields.at[0, row], near.at[side, 0:levs, :]),
             (fields.at[1, row], near.at[side, levs : 2 * levs, :]),
-            (courant.at[1, pl.ds((1, 0)[side], 3)], cy_halo.at[side]),
-            (courant.at[0, pl.ds((2, 0)[side], 2)], cx_halo.at[side]),
-            (far_stage.at[pl.ds((0, 1)[side], 3)], far.at[side]),
+            (courant.at[1, pl.ds((rows - 2, 0)[side], 2)], cy_halo.at[side]),
+            (stage.at[side, 0], far.at[side, 0]),
+            (stage.at[side, pl.ds(1, 2)], far.at[side, pl.ds(1, 2)]),
         ]
         return [
             pltpu.make_async_remote_copy(
@@ -153,7 +153,6 @@
         def _():
             near[side] = jnp.zeros(near.shape[1:], F32)
             far[side] = jnp.zeros(far.shape[1:], BF16)
-            cx_halo[side] = jnp.zeros(cx_halo.shape[1:], BF16)
             cy_halo[side] = jnp.zeros(cy_halo.shape[1:], BF16)
 
     def both(x):
@@ -161,72 +160,77 @@
 
     def cy_row(r):
         if r < 0:
-            return both(cy_halo[0, r + 3].astype(F32))
+            return both(cy_halo[0, r + 2].astype(F32))
         if r >= rows:
             return both(cy_halo[1, r - rows].astype(F32))
         return both(cv[1, r].astype(F32))
 
-    def cx_row(r):
-        if r < 0:
-            return both(cx_halo[0, r + 2].astype(F32))
-        if r >= rows:
-            return both(cx_halo[1, r - rows].astype(F32))
-        return both(cv[0, r].astype(F32))
-
-    def u_row(r, at=slice(None)):
-        if r == -1:
-            return near[0, :, at]
-        if r < 0:
-            return far[0, r + 4, :, at].astype(F32)
-        if r == rows:
-            return near[1, :, at]
-        if r > rows:
-            return far[1, r - rows - 1, :, at].astype(F32)
-        return u[r, :, at]
-
     def v_row(r, at=slice(None)):
         return v[r + 2, :, at]
 
     def set_coef_x(r):
-        cx = cx_row(r)
-        coef_x[r + 2] = (cx + pltpu.roll(cx, length - 1, 1)) * (1.0 / 24.0)
+        cx = both(cv[0, r].astype(F32))
+        coef_x[r] = (cx + pltpu.roll(cx, length - 1, 1)) * (1.0 / 24.0)
 
     def set_coef_y(r):
-        coef_y[r + 3] = (cy_row(r) + cy_row(r + 1)) * (1.0 / 24.0)
-
-    def meridional(source, goal, shift, first, count, start, piece):
-        at = pl.ds(pl.multiple_of(start, 128), piece)
-        full = [source(r, at) for r in range(first - 2, first + count + 2)]
+        coef_y[r + 2] = (cy_row(r) + cy_row(r + 1)) * (1.0 / 24.0)
+
+    def pieces(body, piece=512):
+        @pl.loop(0, length // piece)
+        def _(c):
+            body(pl.ds(pl.multiple_of(c * piece, 128), piece))
+
+    def own_part(at):
+        u0, u1, u2, u3 = (u[r, :, at] for r in range(4))
+        low = coef_y[2, :, at] * (7.0 * (u0 + u1) - u2)
+        middle = coef_y[3, :, at] * (7.0 * (u1 + u2) - (u0 + u3))
+        high = coef_y[4, :, at] * (7.0 * (u2 + u3) - u1)
+        z0, z1 = z[0, :, at] - low, z[1, :, at] - middle + low
+        z2, z3 = z[2, :, at] - high + middle, z[3, :, at] + high
+        z[0, :, at], z[1, :, at], z[2, :, at], z[3, :, at] = z0, z1, z2, z3
+        stage[0, 1, :, at] = (z3 - u3).astype(BF16)
+        stage[0, 2, :, at] = z2.astype(BF16)
+        stage[1, 1, :, at] = (z0 - u0).astype(BF16)
+        stage[1, 2, :, at] = z1.astype(BF16)
+
+    def halo_part(side, at):
+        edge, inner, sign = ((0, 1, 1.0), (rows - 1, rows - 2, -1.0))[side]
+        outer, outermost = ((1, 0), (rows + 2, rows + 3))[side]
+        beyond, shared, inside = ((0, 1, 2), (rows + 2, rows + 1, rows))[side]
+        n, f = near[side, :, at], far[side, 0, :, at].astype(F32)
+        change, value = far[side, 1, :, at].astype(F32), far[side, 2, :, at].astype(F32)
+        flux = coef_y[shared, :, at] * (7.0 * (n + u[edge, :, at]) - (f + u[inner, :, at]))
+        mine = coef_y[inside, :, at] * n
+        theirs = coef_y[beyond, :, at] * u[edge, :, at]
+        v[edge + 2, :, at] = z[edge, :, at] + sign * (mine + flux)
+        v[inner + 2, :, at] = z[inner, :, at] - sign * mine
+        v[outer, :, at] = n + change - sign * (flux + theirs)
+        v[outermost, :, at] = value + sign * theirs
+
+    def second_part(at):
+        full = [v_row(r, at) for r in range(-2, rows + 2)]
         before = None
-        for n in range(count + 1):
+        for n in range(rows + 1):
             a, b, d, e = full[n : n + 4]
-            r = first + n - 1
-            flux = coef_y[r + 3, :, at] * (7.0 * (b + d) - (a + e))
+            flux = coef_y[n + 1, :, at] * (7.0 * (b + d) - (a + e))
             if before is not None:
-                goal[r + shift, :, at] = z[r + 2, :, at] - (flux - before)
+                u[n - 1, :, at] = z[n - 1, :, at] - (flux - before)
             before = flux
 
     def first_substep(side):
-        half = rows // 2
         if side == 0:
-            group, outer, faces, other = -2, (-2, -1), (-3, -2, -1), ilat - 1
+            group, outer, faces, other = -2, (0, 1), (-2, -1), ilat - 1
         else:
-            group, outer, other = half, (rows, rows + 1), ilat + 1
-            faces = (rows - 1, rows, rows + 1)
+            group, outer, other = rows // 2, (rows + 2, rows + 3), ilat + 1
+            faces = (rows - 1, rows)
         for r in faces:
             set_coef_y(r)
-        for r in outer:
-            set_coef_x(r)
-            z[r + 2] = zonal(u_row(r), coef_x[r + 2])
-
-        @pl.loop(0, length // 512)
-        def _(c):
-            meridional(u_row, v, 2, group, rows, c * 512, 512)
+        pieces(functools.partial(halo_part, side))
 
         @pl.when(jnp.logical_not(there[1 - side]))
         def _():
             for r in outer:
-                v[r + 2] = jnp.zeros(v.shape[1:], F32)
+                v[r] = jnp.zeros(v.shape[1:], F32)
 
         def band_is_polar(band):
             return jnp.logical_or(band < polar, band >= n_lat - polar)
@@ -236,7 +240,7 @@
             low_pass(v, group + 2, group)
 
         for r in range(max(group, 0), min(group + rows, rows)):
-            z[r + 2] = zonal(v_row(r), coef_x[r + 2])
+            z[r] = zonal(v_row(r), coef_x[r])
 
     def low_pass(ref, base, first):
         x = jnp.concatenate([ref[base + j] for j in range(rows)], axis=0)
@@ -333,23 +337,26 @@
         column_copy(n_y - 1, 1 - parity).start()
         recv[ilev] = send[ilev]
 
-    halo_start(0, 4)
+    halo_start(0, 3)
     for load in loads[3:]:
         load.start()
     for load in loads[:2]:
         load.wait()
+    stage[0, 0] = u[rows - 2].astype(BF16)
+    stage[1, 0] = u[1].astype(BF16)
+    halo_start(3, 4)
+    loads[2].wait()
     for r in range(rows):
-        far_stage[r] = u[r].astype(BF16)
+        set_coef_x(r)
+        z[r] = zonal(u[r], coef_x[r])
+    for r in range(rows - 1):
+        set_coef_y(r)
+    pieces(own_part)
     halo_start(4, 5)
     tell(ring_one, lev=level(1, parity))
     tell(ring_one, lev=level(-1, parity))
-    for load in loads[2:]:
+    for load in loads[3:]:
         load.wait()
-    for r in range(rows):
-        set_coef_x(r)
-        z[r + 2] = zonal(u[r], coef_x[r + 2])
-    for r in range(rows - 1):
-        set_coef_y(r)
     write_maps(n_lev, levs, wv, maps)
     halo_wait(1)
     first_substep(1)
@@ -363,16 +370,13 @@
 
     @pl.when(is_polar)
     def _():
-        @pl.loop(0, length // 512)
-        def _(c):
-            meridional(v_row, u, 0, 0, rows, c * 512, 512)
-
+        pieces(second_part)
         low_pass(u, 0, 0)
         columns(lambda e: None)
 
     @pl.when(jnp.logical_not(is_polar))
     def _():
-        columns(lambda e: meridional(v_row, u, 0, 0, rows, e * width, width))
+        columns(lambda e: second_part(pl.ds(pl.multiple_of(e * width, 128), width)))
 
     for side in (0, 1):
 
@@ -431,9 +435,11 @@
         if f < 2:
             out_v[f, j, :, 0:128] = first
             out_v[f, j, :, 128:192] = second[:, 0:64]
+            pltpu.make_async_copy(out_v.at[f, j], out.at[f, j], out_sem.at[f, j]).start()
         else:
             geo_v[j, :, 0:128] = first
             geo_v[j, :, 128:192] = second[:, 0:64]
+            pltpu.make_async_copy(geo_v.at[j], geo.at[j], geo_sem.at[j]).start()
 
     @pl.when(parity == 0)
     def _():
@@ -465,11 +471,6 @@
                 main = pltpu.roll(main, 64, 1)
                 put(j, f, jnp.where(low_out, side, main), main)
 
-    for j in range(rows):
-        copies = [pltpu.make_async_copy(out_v.at[f, j], out.at[f, j], out_sem.at[f, j]) for f in range(2)]
-        copies.append(pltpu.make_async_copy(geo_v.at[j], geo.at[j], geo_sem.at[j]))
-        for copy in copies:
-            copy.start()
     for j in range(rows):
         for f in range(2):
             pltpu.make_async_copy(out_v.at[f, j], out.at[f, j], out_sem.at[f, j]).wait()
@@ -506,14 +507,13 @@
                 pltpu.VMEM(turn.shape, F32),
                 pltpu.VMEM((rows, 2 * levs, length), F32),
                 pltpu.VMEM((rows + 4, 2 * levs, length), F32),
-                pltpu.VMEM((rows + 4, 2 * levs, length), F32),
-                pltpu.VMEM((rows + 4, 2 * levs, length), F32),
-                pltpu.VMEM((rows + 5, 2 * levs, length), F32),
+                pltpu.VMEM((rows, 2 * levs, length), F32),
+                pltpu.VMEM((rows, 2 * levs, length), F32),
+                pltpu.VMEM((rows + 3, 2 * levs, length), F32),
                 pltpu.VMEM((2, 2 * levs, length), F32),
                 pltpu.VMEM((2, 3, 2 * levs, length), BF16),
-                pltpu.VMEM((rows, 2 * levs, length), BF16),
+                pltpu.VMEM((2, 3, 2 * levs, length), BF16),
                 pltpu.VMEM((2, 2, levs, length), BF16),
-                pltpu.VMEM((2, 3, levs, length), BF16),
                 pltpu.VMEM((n_lev, tiles + 1, 2 * levs, 128), jnp.int16),
                 dma((9,)),
                 dma((2, 5)),

time: 33.7 us -> 31.5 us (0.935)
  Pallas kernels: 32.9 us -> 30.7 us
    pallas_call x1, Pallas kernels: 31.3 us -> 29.2 us  [shards(): pl.pallas_call(functools.partial(transport, n_lat, n_lev, 16 // rows), na...]
where the time goes in v4:
time: 31.5 us; the launch traced here: 31.4 us
  Pallas kernels  30.7 us (97%)
  between operations  0.64 us (2%)
    pallas_call x1, Pallas kernels, shards(): pl.pallas_call(functools.partial(transport, n_lat, n_lev, 16 // rows), na...  29.2 us
    pallas_call x1, Pallas kernels, shards(): pl.pallas_call(remap, name='remap', out_shape=(jax.ShapeDtypeStruct((2, r...  1.49 us

profile of v4, /device:TPU:7, one launch (start us, length us, event | category | flops | bytes accessed | tf_op | source)
XLA Modules:
  0.0 31.4 jit_solution(13910719678584396367)
XLA Ops:
  0.6 29.2 %transport.1 = (s16[16,7,8,128]{3,2,1,0:T(8,128)(2,1)S(1)}, bf16[2,192,128]{2,1,0:T(8,128)(2,1)S(1)}, f32[4,384]{1,0:T(4,128)S(1)}) custom-call(f32[2,4,4,3072]{3,2,1,0:T(4,128)} %fields.1, bf16[2,4,4,3072]{3,2,1,0:T(4,128)(2,1)} %courant.1, s32[128]{0:T(128)} %cutoffs.1, f32[4,3072]{1,0:T(4,128)} %surface.1, f32[64,64]{1,0:T(8,128)} %weights.1, ...), custom_call_target="tpu_custom_call" | custom-call | tf_op jit(solution)/shard_map/transport/pallas_call | solution.py:491
  29.9 1.5 %remap.1 = (f32[2,4,64,192]{3,2,1,0:T(8,128)}, f32[4,64,192]{2,1,0:T(8,128)}) custom-call(s16[16,7,8,128]{3,2,1,0:T(8,128)(2,1)S(1)} %get-tuple-element.5.recv, bf16[2,192,128]{2,1,0:T(8,128)(2,1)S(1)} %get-tuple-element.6.maps, f32[4,384]{1,0:T(4,128)S(1)} %get-tuple-element.7.surf), custom_call_target="tpu_custom_call" | custom-call | tf_op jit(solution)/shard_map/remap/pallas_call | solution.py:531

commit v5 on v4

--- a/solution.py
+++ b/solution.py
@@ -12,7 +12,6 @@
 KMAX = 128
 SEG = 256
 CODE_MAX = 32767.0
-STEPS = 256.0
 ROUNDER = 1.5 * 2.0**23
 F32 = jnp.float32
 BF16 = jnp.bfloat16
@@ -59,10 +58,10 @@
 def transport(
     n_lat, n_lev, polar,
     fields, courant, cutoffs, surface, weights, fwd, inv, turn,
-    recv, maps, surf,
+    x_high, x_low, maps, surf,
     cv, cut, wv, fwd_v, inv_v, turn_v,
-    u, v, z, coef_x, coef_y, near, far, stage, cy_halo, send,
-    in_sem, halo_send, halo_recv, a2a_send, a2a_recv,
+    u, v, z, coef_x, coef_y, near, near_sent, near_got, near_scale, far, stage, cy_halo, send, recv, send_scale, recv_scale,
+    in_sem, halo_send, halo_recv, a2a_send, a2a_recv, scale_sent, scale_got,
     ring_one, ring_two,
 ):
     ilat, ilev = lax.axis_index("lat"), lax.axis_index("lev")
@@ -116,11 +115,10 @@
     pl.semaphore_wait(barrier, 5 + neighbours)
 
     def halo_copies(side):
-        row = (rows - 1, 0)[side]
         pieces = [
-            (fields.at[0, row], near.at[side, 0:levs, :]),
-            (fields.at[1, row], near.at[side, levs : 2 * levs, :]),
             (courant.at[1, pl.ds((rows - 2, 0)[side], 2)], cy_halo.at[side]),
+            (near_scale.at[0, side], near_scale.at[1, side]),
+            (near_sent.at[side], near_got.at[side]),
             (stage.at[side, 0], far.at[side, 0]),
             (stage.at[side, pl.ds(1, 2)], far.at[side, pl.ds(1, 2)]),
         ]
@@ -151,7 +149,8 @@
 
         @pl.when(jnp.logical_not(there[1 - side]))
         def _():
-            near[side] = jnp.zeros(near.shape[1:], F32)
+            near_got[side] = jnp.zeros(near_got.shape[1:], jnp.int16)
+            near_scale[1, side] = jnp.zeros(near_scale.shape[2:], F32)
             far[side] = jnp.zeros(far.shape[1:], BF16)
             cy_halo[side] = jnp.zeros(cy_halo.shape[1:], BF16)
 
@@ -164,6 +163,25 @@
         if r >= rows:
             return both(cy_halo[1, r - rows].astype(F32))
         return both(cv[1, r].astype(F32))
+
+    def spans():
+        return [slice(t * 128, (t + 1) * 128) for t in range(length // 128)]
+
+    def send_near(side):
+        row = (rows - 1, 0)[side]
+        most = jnp.full((2 * levs, 128), 1e-30, F32)
+        for at in spans():
+            most = jnp.maximum(most, jnp.abs(u[row, :, at]))
+        most = jnp.max(most, axis=0, keepdims=True)
+        near_scale[0, side] = most * (1.0 / CODE_MAX)
+        to_code = CODE_MAX / most
+        for at in spans():
+            code = (u[row, :, at] * to_code + ROUNDER) - ROUNDER
+            near_sent[side, :, at] = code.astype(jnp.int32).astype(jnp.int16)
+
+    def take_near(side):
+        for at in spans():
+            near[side, :, at] = near_got[side, :, at].astype(jnp.int32).astype(F32) * near_scale[1, side]
 
     def v_row(r, at=slice(None)):
         return v[r + 2, :, at]
@@ -223,6 +241,7 @@
         else:
             group, outer, other = rows // 2, (rows + 2, rows + 3), ilat + 1
             faces = (rows - 1, rows)
+        take_near(side)
         for r in faces:
             set_coef_y(r)
         pieces(functools.partial(halo_part, side))
@@ -284,12 +303,12 @@
         most = jnp.abs(parts[0])
         for part in parts[1:]:
             most = jnp.maximum(most, jnp.abs(part))
-        power = jnp.ceil(jnp.log2(jnp.maximum(most, 1e-30)) * STEPS + 0.01)
-        to_code = jnp.exp2(power * (-1.0 / STEPS)) * CODE_MAX
+        most = jnp.maximum(jnp.max(most, axis=0, keepdims=True), 1e-30)
+        to_code = CODE_MAX / most
+        send_scale[slot] = most * (1.0 / CODE_MAX)
         for a, part in enumerate(parts):
-            code = jnp.clip((part * to_code + ROUNDER) - ROUNDER, -CODE_MAX, CODE_MAX)
+            code = (part * to_code + ROUNDER) - ROUNDER
             send[slot, a] = code.astype(jnp.int32).astype(jnp.int16)
-        send[slot, tiles] = power.astype(jnp.int32).astype(jnp.int16)
 
     def pack(e):
         def tile(j, t):
@@ -308,20 +327,45 @@
         half = lax.div(step + 1, 2)
         return lax.rem(y + n_y // 2 + jnp.where(lax.rem(step, 2) == 1, -half, half), n_y)
 
-    def column_copy(step, core):
+    def column_copies(step, core):
         other = target(step) * 2 + core
-        return pltpu.make_async_remote_copy(
-            src_ref=send.at[other], dst_ref=recv.at[ilev],
-            send_sem=a2a_send.at[step, core], recv_sem=a2a_recv.at[step, parity],
-            device_id={"lev": other}, device_id_type=MESH,
-        )
-
-    def column_arrival(step, core):
-        return pltpu.make_async_remote_copy(
-            src_ref=send.at[0], dst_ref=recv.at[ilev],
-            send_sem=a2a_send.at[step, core], recv_sem=a2a_recv.at[step, core],
-            device_id={"lev": ilev}, device_id_type=MESH,
-        )
+        return [
+            pltpu.make_async_remote_copy(
+                src_ref=source.at[other], dst_ref=goal.at[ilev],
+                send_sem=sent.at[step, core], recv_sem=got.at[step, parity],
+                device_id={"lev": other}, device_id_type=MESH,
+            )
+            for source, goal, sent, got in (
+                (send_scale, recv_scale, scale_sent, scale_got),
+                (send, recv, a2a_send, a2a_recv),
+            )
+        ]
+
+    def column_start(step, core):
+        for copy in column_copies(step, core):
+            copy.start()
+
+    def column_wait(step, core):
+        for source, goal, sent, got in (
+            (send_scale, recv_scale, scale_sent, scale_got),
+            (send, recv, a2a_send, a2a_recv),
+        ):
+            pltpu.make_async_remote_copy(
+                src_ref=source.at[0], dst_ref=goal.at[ilev],
+                send_sem=sent.at[step, core], recv_sem=got.at[step, core],
+                device_id={"lev": ilev}, device_id_type=MESH,
+            ).wait_recv()
+
+    def decode(chip):
+        for a in range(tiles):
+            parts = []
+            for core in range(2):
+                code = recv[2 * chip + core, a].astype(jnp.int32).astype(F32)
+                parts.append(code * recv_scale[2 * chip + core])
+            high, low = halves(jnp.concatenate(parts, axis=0))
+            at = pl.ds(pl.multiple_of(chip * 4 * levs, 4 * levs), 4 * levs)
+            x_high[at, a * 128 : (a + 1) * 128] = high
+            x_low[at, a * 128 : (a + 1) * 128] = low
 
     def columns(before):
         @pl.loop(0, n_y - 1)
@@ -329,19 +373,23 @@
             e = target(step)
             before(e)
             pack(e)
-            column_copy(step, 0).start()
-            column_copy(step, 1).start()
+            column_start(step, 0)
+            column_start(step, 1)
 
         before(y)
         pack(y)
-        column_copy(n_y - 1, 1 - parity).start()
+        column_start(n_y - 1, 1 - parity)
         recv[ilev] = send[ilev]
-
-    halo_start(0, 3)
+        recv_scale[ilev] = send_scale[ilev]
+
+    halo_start(0, 1)
     for load in loads[3:]:
         load.start()
     for load in loads[:2]:
         load.wait()
+    send_near(0)
+    send_near(1)
+    halo_start(1, 3)
     stage[0, 0] = u[rows - 2].astype(BF16)
     stage[1, 0] = u[1].astype(BF16)
     halo_start(3, 4)
@@ -385,14 +433,24 @@
             for copy in halo_copies(side):
                 copy.wait_send()
 
+    column_wait(n_y - 1, 1 - parity)
+    decode(y)
+
+    @pl.loop(1, n_y)
+    def _(lap):
+        step = n_y - 1 - lap
+        column_wait(step, 0)
+        column_wait(step, 1)
+        decode(lax.rem(2 * y + n_y - target(step), n_y))
+
     @pl.loop(0, n_y - 1)
     def _(step):
         for core in range(2):
-            column_copy(step, core).wait_send()
-            column_arrival(step, core).wait_recv()
-
-    column_copy(n_y - 1, 1 - parity).wait_send()
-    column_arrival(n_y - 1, 1 - parity).wait_recv()
+            for copy in column_copies(step, core):
+                copy.wait_send()
+
+    for copy in column_copies(n_y - 1, 1 - parity):
+        copy.wait_send()
 
 
 def write_maps(n_lev, levs, wv, maps):
@@ -414,21 +472,13 @@
     maps[1, 2 * count : 3 * count, :] = jnp.zeros((count, depth), BF16)
 
 
-def remap(recv, maps, surf, out, geo, out_v, geo_v, out_sem, geo_sem):
-    n_lev, tiles, depth_rows = recv.shape[0], recv.shape[1] - 1, recv.shape[2]
+def remap(x_high, x_low, maps, surf, out, geo, out_v, geo_v, out_sem, geo_sem):
     rows = surf.shape[0]
     count = maps.shape[1] // 3
-    depth = n_lev * depth_rows
     parity = lax.rem(lax.axis_index("lev"), 2)
-    scale = jnp.exp2(recv[:, tiles].astype(jnp.int32).astype(F32) * (1.0 / STEPS))
-    scale = (scale * (1.0 / CODE_MAX)).reshape(depth, 128)
-    values = [
-        recv[:, a].astype(jnp.int32).astype(F32).reshape(depth, 128) * scale for a in range(tiles)
-    ]
-    x_high, x_low = halves(jnp.concatenate(values, axis=1))
-    y = jnp.dot(maps[0], x_high, preferred_element_type=F32)
-    y += jnp.dot(maps[0], x_low, preferred_element_type=F32)
-    y += jnp.dot(maps[1], x_high, preferred_element_type=F32)
+    y = jnp.dot(maps[0], x_high[...], preferred_element_type=F32)
+    y += jnp.dot(maps[0], x_low[...], preferred_element_type=F32)
+    y += jnp.dot(maps[1], x_high[...], preferred_element_type=F32)
     low_out = lax.broadcasted_iota(jnp.int32, (count, 128), 1) < 64
 
     def put(j, f, first, second):
@@ -488,16 +538,17 @@
         hbm_spec = pl.BlockSpec(memory_space=pltpu.HBM)
         vmem_spec = pl.BlockSpec(memory_space=pltpu.VMEM)
         dma = pltpu.SemaphoreType.DMA
-        recv, maps, surf = pl.pallas_call(
+        parts = pl.pallas_call(
             functools.partial(transport, n_lat, n_lev, 16 // rows),
             name="transport",
             out_shape=(
-                pltpu.VMEM((n_lev, tiles + 1, 2 * levs, 128), jnp.int16),
+                pltpu.VMEM((2 * count, tiles * 128), BF16),
+                pltpu.VMEM((2 * count, tiles * 128), BF16),
                 pltpu.VMEM((2, 3 * count, 2 * count), BF16),
                 pltpu.VMEM((rows, 384), F32),
             ),
             in_specs=[hbm_spec] * 8,
-            out_specs=(vmem_spec,) * 3,
+            out_specs=(vmem_spec,) * 4,
             scratch_shapes=[
                 pltpu.VMEM(courant.shape, BF16),
                 pltpu.SMEM(cutoffs.shape, jnp.int32),
@@ -511,13 +562,21 @@
                 pltpu.VMEM((rows, 2 * levs, length), F32),
                 pltpu.VMEM((rows + 3, 2 * levs, length), F32),
                 pltpu.VMEM((2, 2 * levs, length), F32),
+                pltpu.VMEM((2, 2 * levs, length), jnp.int16),
+                pltpu.VMEM((2, 2 * levs, length), jnp.int16),
+                pltpu.VMEM((2, 2, 1, 128), F32),
                 pltpu.VMEM((2, 3, 2 * levs, length), BF16),
                 pltpu.VMEM((2, 3, 2 * levs, length), BF16),
                 pltpu.VMEM((2, 2, levs, length), BF16),
-                pltpu.VMEM((n_lev, tiles + 1, 2 * levs, 128), jnp.int16),
+                pltpu.VMEM((n_lev, tiles, 2 * levs, 128), jnp.int16),
+                pltpu.VMEM((n_lev, tiles, 2 * levs, 128), jnp.int16),
+                pltpu.VMEM((n_lev, 1, 128), F32),
+                pltpu.VMEM((n_lev, 1, 128), F32),
                 dma((9,)),
                 dma((2, 5)),
                 dma((2, 5)),
+                dma((n_lev // 2, 2)),
+                dma((n_lev // 2, 2)),
                 dma((n_lev // 2, 2)),
                 dma((n_lev // 2, 2)),
                 pltpu.SemaphoreType.REGULAR,
@@ -535,7 +594,7 @@
                 jax.ShapeDtypeStruct((2, rows, count, columns), F32),
                 jax.ShapeDtypeStruct((rows, count, columns), F32),
             ),
-            in_specs=[vmem_spec] * 3,
+            in_specs=[vmem_spec] * 4,
             out_specs=(hbm_spec, hbm_spec),
             scratch_shapes=[
                 pltpu.VMEM((2, rows, count, columns), F32),
@@ -544,7 +603,7 @@
                 dma((rows,)),
             ],
             compiler_params=pltpu.CompilerParams(vmem_limit_bytes=24 << 20),
-        )(recv, maps, surf)
+        )(*parts)
 
     return jax.shard_map(
         shards,

time: 31.5 us -> 30.4 us (0.965)
  Pallas kernels: 30.7 us -> 29.6 us
    pallas_call x1, Pallas kernels: 29.2 us -> 28.2 us  [shards(): pl.pallas_call(functools.partial(transport, n_lat, n_lev, 16 // rows), na...]
where the time goes in v5:
time: 30.4 us; the launch traced here: 30.2 us
  Pallas kernels  29.6 us (97%)
  between operations  0.64 us (2%)
    pallas_call x1, Pallas kernels, shards(): pl.pallas_call(functools.partial(transport, n_lat, n_lev, 16 // rows), na...  28.2 us
    pallas_call x1, Pallas kernels, shards(): pl.pallas_call(remap, name='remap', out_shape=(jax.ShapeDtypeStruct((2, r...  1.43 us

profile of v5, /device:TPU:7, one launch (start us, length us, event | category | flops | bytes accessed | tf_op | source)
XLA Modules:
  0.0 30.2 jit_solution(14699913422840423188)
XLA Ops:
  0.6 28.2 %transport.1 = (bf16[128,768]{1,0:T(8,128)(2,1)S(1)}, bf16[128,768]{1,0:T(8,128)(2,1)S(1)}, bf16[2,192,128]{2,1,0:T(8,128)(2,1)S(1)}, f32[4,384]{1,0:T(4,128)S(1)}) custom-call(f32[2,4,4,3072]{3,2,1,0:T(4,128)} %fields.1, bf16[2,4,4,3072]{3,2,1,0:T(4,128)(2,1)} %courant.1, s32[128]{0:T(128)} %cutoffs.1, f32[4,3072]{1,0:T(4,128)} %surface.1, ...), custom_call_target="tpu_custom_call" | custom-call | tf_op jit(solution)/shard_map/transport/pallas_call | solution.py:541
  28.8 1.4 %remap.1 = (f32[2,4,64,192]{3,2,1,0:T(8,128)}, f32[4,64,192]{2,1,0:T(8,128)}) custom-call(bf16[128,768]{1,0:T(8,128)(2,1)S(1)} %get-tuple-element.6.x_high, bf16[128,768]{1,0:T(8,128)(2,1)S(1)} %get-tuple-element.7.x_low, bf16[2,192,128]{2,1,0:T(8,128)(2,1)S(1)} %get-tuple-element.8.maps, f32[4,384]{1,0:T(4,128)S(1)} %get-tuple-element.9.surf), custom_call_target="tpu_custom_call" | custom-call | tf_op jit(solution)/shard_map/remap/pallas_call | solution.py:590

commit v6 on v5

--- a/solution.py
+++ b/solution.py
@@ -116,7 +116,7 @@
 
     def halo_copies(side):
         pieces = [
-            (courant.at[1, pl.ds((rows - 2, 0)[side], 2)], cy_halo.at[side]),
+            (cv.at[1, pl.ds((rows - 2, 0)[side], 2)], cy_halo.at[side]),
             (near_scale.at[0, side], near_scale.at[1, side]),
             (near_sent.at[side], near_got.at[side]),
             (stage.at[side, 0], far.at[side, 0]),
@@ -382,6 +382,7 @@
         recv[ilev] = send[ilev]
         recv_scale[ilev] = send_scale[ilev]
 
+    loads[2].wait()
     halo_start(0, 1)
     for load in loads[3:]:
         load.start()
@@ -393,7 +394,6 @@
     stage[0, 0] = u[rows - 2].astype(BF16)
     stage[1, 0] = u[1].astype(BF16)
     halo_start(3, 4)
-    loads[2].wait()
     for r in range(rows):
         set_coef_x(r)
         z[r] = zonal(u[r], coef_x[r])

time: 30.4 us -> 30.2 us (level)
  no operation moved by 1% of the time
where the time goes in v6:
time: 30.2 us; the launch traced here: 30 us
  Pallas kernels  29.4 us (97%)
  between operations  0.64 us (2%)
    pallas_call x1, Pallas kernels, shards(): pl.pallas_call(functools.partial(transport, n_lat, n_lev, 16 // rows), na...  27.9 us
    pallas_call x1, Pallas kernels, shards(): pl.pallas_call(remap, name='remap', out_shape=(jax.ShapeDtypeStruct((2, r...  1.44 us

profile of v6, /device:TPU:7, one launch (start us, length us, event | category | flops | bytes accessed | tf_op | source)
XLA Modules:
  0.0 30.0 jit_solution(15848212062167901872)
XLA Ops:
  0.6 27.9 %transport.1 = (bf16[128,768]{1,0:T(8,128)(2,1)S(1)}, bf16[128,768]{1,0:T(8,128)(2,1)S(1)}, bf16[2,192,128]{2,1,0:T(8,128)(2,1)S(1)}, f32[4,384]{1,0:T(4,128)S(1)}) custom-call(f32[2,4,4,3072]{3,2,1,0:T(4,128)} %fields.1, bf16[2,4,4,3072]{3,2,1,0:T(4,128)(2,1)} %courant.1, s32[128]{0:T(128)} %cutoffs.1, f32[4,3072]{1,0:T(4,128)} %surface.1, ...), custom_call_target="tpu_custom_call" | custom-call | tf_op jit(solution)/shard_map/transport/pallas_call | solution.py:541
  28.6 1.4 %remap.1 = (f32[2,4,64,192]{3,2,1,0:T(8,128)}, f32[4,64,192]{2,1,0:T(8,128)}) custom-call(bf16[128,768]{1,0:T(8,128)(2,1)S(1)} %get-tuple-element.6.x_high, bf16[128,768]{1,0:T(8,128)(2,1)S(1)} %get-tuple-element.7.x_low, bf16[2,192,128]{2,1,0:T(8,128)(2,1)S(1)} %get-tuple-element.8.maps, f32[4,384]{1,0:T(4,128)S(1)} %get-tuple-element.9.surf), custom_call_target="tpu_custom_call" | custom-call | tf_op jit(solution)/shard_map/remap/pallas_call | solution.py:590

commit v7 on v6

--- a/solution.py
+++ b/solution.py
@@ -86,6 +86,9 @@
         pltpu.make_async_copy(turn, turn_v, in_sem.at[8]),
     ]
 
+    for n in (2, 0, 1):
+        loads[n].start()
+
     has_minus, has_plus = ilat > 0, ilat < n_lat - 1
     barrier = pltpu.get_barrier_semaphore()
 
@@ -107,9 +110,6 @@
         tell(barrier, lev=level(1, core))
         tell(barrier, lev=level(-1, core))
     tell(barrier, lev=level(0, 1 - parity))
-
-    for load in loads[:3]:
-        load.start()
 
     neighbours = has_minus.astype(jnp.int32) + has_plus.astype(jnp.int32)
     pl.semaphore_wait(barrier, 5 + neighbours)
@@ -141,18 +141,20 @@
                 for copy in halo_copies(side)[first:last]:
                     copy.start()
 
-    def halo_wait(side):
+    def halo_wait(side, first, last):
         @pl.when(there[1 - side])
         def _():
-            for copy in halo_copies(side):
+            for copy in halo_copies(side)[first:last]:
                 copy.wait_recv()
 
-        @pl.when(jnp.logical_not(there[1 - side]))
-        def _():
-            near_got[side] = jnp.zeros(near_got.shape[1:], jnp.int16)
-            near_scale[1, side] = jnp.zeros(near_scale.shape[2:], F32)
-            far[side] = jnp.zeros(far.shape[1:], BF16)
-            cy_halo[side] = jnp.zeros(cy_halo.shape[1:], BF16)
+        if first == 0:
+
+            @pl.when(jnp.logical_not(there[1 - side]))
+            def _():
+                near_got[side] = jnp.zeros(near_got.shape[1:], jnp.int16)
+                near_scale[1, side] = jnp.zeros(near_scale.shape[2:], F32)
+                far[side] = jnp.zeros(far.shape[1:], BF16)
+                cy_halo[side] = jnp.zeros(cy_halo.shape[1:], BF16)
 
     def both(x):
         return jnp.concatenate([x, x], axis=0)
@@ -211,55 +213,66 @@
         stage[1, 1, :, at] = (z0 - u0).astype(BF16)
         stage[1, 2, :, at] = z1.astype(BF16)
 
-    def halo_part(side, at):
-        edge, inner, sign = ((0, 1, 1.0), (rows - 1, rows - 2, -1.0))[side]
-        outer, outermost = ((1, 0), (rows + 2, rows + 3))[side]
-        beyond, shared, inside = ((0, 1, 2), (rows + 2, rows + 1, rows))[side]
+    places = (
+        ((1, 0), (0, 1), (0, 1, 2), 1.0),
+        ((rows + 2, rows + 3), (rows - 1, rows - 2), (rows + 2, rows + 1, rows), -1.0),
+    )
+
+    def inner_part(side, at):
+        (outer, outermost), (edge, inner), (beyond, shared, inside), sign = places[side]
         n, f = near[side, :, at], far[side, 0, :, at].astype(F32)
-        change, value = far[side, 1, :, at].astype(F32), far[side, 2, :, at].astype(F32)
         flux = coef_y[shared, :, at] * (7.0 * (n + u[edge, :, at]) - (f + u[inner, :, at]))
         mine = coef_y[inside, :, at] * n
         theirs = coef_y[beyond, :, at] * u[edge, :, at]
         v[edge + 2, :, at] = z[edge, :, at] + sign * (mine + flux)
         v[inner + 2, :, at] = z[inner, :, at] - sign * mine
-        v[outer, :, at] = n + change - sign * (flux + theirs)
-        v[outermost, :, at] = value + sign * theirs
-
-    def second_part(at):
-        full = [v_row(r, at) for r in range(-2, rows + 2)]
+        v[outer, :, at] = n - sign * (flux + theirs)
+        v[outermost, :, at] = sign * theirs
+
+    def outer_part(side, at):
+        outer, outermost = places[side][0]
+        v[outer, :, at] += far[side, 1, :, at].astype(F32)
+        v[outermost, :, at] += far[side, 2, :, at].astype(F32)
+
+    def second_part(first, at):
+        full = [v_row(r, at) for r in range(first - 2, first + 4)]
         before = None
-        for n in range(rows + 1):
+        for n in range(3):
             a, b, d, e = full[n : n + 4]
-            flux = coef_y[n + 1, :, at] * (7.0 * (b + d) - (a + e))
+            r = first + n - 1
+            flux = coef_y[r + 2, :, at] * (7.0 * (b + d) - (a + e))
             if before is not None:
-                u[n - 1, :, at] = z[n - 1, :, at] - (flux - before)
+                u[r, :, at] = z[r, :, at] - (flux - before)
             before = flux
 
-    def first_substep(side):
-        if side == 0:
-            group, outer, faces, other = -2, (0, 1), (-2, -1), ilat - 1
-        else:
-            group, outer, other = rows // 2, (rows + 2, rows + 3), ilat + 1
-            faces = (rows - 1, rows)
+    def band_is_polar(band):
+        return jnp.logical_or(band < polar, band >= n_lat - polar)
+
+    def second_zonal(first):
+        for r in (first, first + 1):
+            z[r] = zonal(v_row(r), coef_x[r])
+
+    def first_inner(side):
         take_near(side)
-        for r in faces:
+        for r in ((-2, -1), (rows - 1, rows))[side]:
             set_coef_y(r)
-        pieces(functools.partial(halo_part, side))
+        pieces(functools.partial(inner_part, side))
+
+    def first_outer(side):
+        pieces(functools.partial(outer_part, side))
+        first = (-2, rows)[side]
 
         @pl.when(jnp.logical_not(there[1 - side]))
         def _():
-            for r in outer:
-                v[r] = jnp.zeros(v.shape[1:], F32)
-
-        def band_is_polar(band):
-            return jnp.logical_or(band < polar, band >= n_lat - polar)
+            for r in (first, first + 1):
+                v[r + 2] = jnp.zeros(v.shape[1:], F32)
+
+        group = (-2, rows // 2)[side]
+        other = ilat + (-1, 1)[side]
 
         @pl.when(jnp.logical_or(band_is_polar(ilat), band_is_polar(other)))
         def _():
             low_pass(v, group + 2, group)
-
-        for r in range(max(group, 0), min(group + rows, rows)):
-            z[r] = zonal(v_row(r), coef_x[r])
 
     def low_pass(ref, base, first):
         x = jnp.concatenate([ref[base + j] for j in range(rows)], axis=0)
@@ -299,40 +312,38 @@
     tiles = rows + rows // 2
     low_lane = lax.broadcasted_iota(jnp.int32, (2 * levs, 128), 1) < 64
 
-    def encode(slot, parts):
+    def encode(slot, half, parts):
         most = jnp.abs(parts[0])
         for part in parts[1:]:
             most = jnp.maximum(most, jnp.abs(part))
         most = jnp.maximum(jnp.max(most, axis=0, keepdims=True), 1e-30)
         to_code = CODE_MAX / most
-        send_scale[slot] = most * (1.0 / CODE_MAX)
+        send_scale[slot, half] = most * (1.0 / CODE_MAX)
         for a, part in enumerate(parts):
             code = (part * to_code + ROUNDER) - ROUNDER
-            send[slot, a] = code.astype(jnp.int32).astype(jnp.int16)
-
-    def pack(e):
+            send[slot, half, a] = code.astype(jnp.int32).astype(jnp.int16)
+
+    def pack(e, half):
         def tile(j, t):
             return u[j, :, pl.ds(pl.multiple_of(e * width + t * 128, 128), 128)]
 
-        first = [tile(j, 0) for j in range(rows)]
-        second = [tile(j, 2) for j in range(rows)]
-        for j in range(0, rows, 2):
-            one, two = tile(j, 1), tile(j + 1, 1)
-            first.append(jnp.where(low_lane, one, pltpu.roll(two, 64, 1)))
-            second.append(jnp.where(low_lane, pltpu.roll(one, 64, 1), two))
-        encode(2 * e, first)
-        encode(2 * e + 1, second)
+        j = 2 * half
+        one, two = tile(j, 1), tile(j + 1, 1)
+        lower = jnp.where(low_lane, one, pltpu.roll(two, 64, 1))
+        upper = jnp.where(low_lane, pltpu.roll(one, 64, 1), two)
+        encode(2 * e, half, [tile(j, 0), tile(j + 1, 0), lower])
+        encode(2 * e + 1, half, [tile(j, 2), tile(j + 1, 2), upper])
 
     def target(step):
         half = lax.div(step + 1, 2)
         return lax.rem(y + n_y // 2 + jnp.where(lax.rem(step, 2) == 1, -half, half), n_y)
 
-    def column_copies(step, core):
+    def column_copies(half, step, core):
         other = target(step) * 2 + core
         return [
             pltpu.make_async_remote_copy(
-                src_ref=source.at[other], dst_ref=goal.at[ilev],
-                send_sem=sent.at[step, core], recv_sem=got.at[step, parity],
+                src_ref=source.at[other, half], dst_ref=goal.at[ilev, half],
+                send_sem=sent.at[half, step, core], recv_sem=got.at[half, step, parity],
                 device_id={"lev": other}, device_id_type=MESH,
             )
             for source, goal, sent, got in (
@@ -341,49 +352,57 @@
             )
         ]
 
-    def column_start(step, core):
-        for copy in column_copies(step, core):
+    def column_start(half, step, core):
+        for copy in column_copies(half, step, core):
             copy.start()
 
-    def column_wait(step, core):
+    def column_wait(half, step, core):
         for source, goal, sent, got in (
             (send_scale, recv_scale, scale_sent, scale_got),
             (send, recv, a2a_send, a2a_recv),
         ):
             pltpu.make_async_remote_copy(
-                src_ref=source.at[0], dst_ref=goal.at[ilev],
-                send_sem=sent.at[step, core], recv_sem=got.at[step, core],
+                src_ref=source.at[0, half], dst_ref=goal.at[ilev, half],
+                send_sem=sent.at[half, step, core], recv_sem=got.at[half, step, core],
                 device_id={"lev": ilev}, device_id_type=MESH,
             ).wait_recv()
 
-    def decode(chip):
-        for a in range(tiles):
+    def decode(half, chip):
+        for n, a in enumerate((2 * half, 2 * half + 1, rows + half)):
             parts = []
             for core in range(2):
-                code = recv[2 * chip + core, a].astype(jnp.int32).astype(F32)
-                parts.append(code * recv_scale[2 * chip + core])
+                code = recv[2 * chip + core, half, n].astype(jnp.int32).astype(F32)
+                parts.append(code * recv_scale[2 * chip + core, half])
             high, low = halves(jnp.concatenate(parts, axis=0))
             at = pl.ds(pl.multiple_of(chip * 4 * levs, 4 * levs), 4 * levs)
             x_high[at, a * 128 : (a + 1) * 128] = high
             x_low[at, a * 128 : (a + 1) * 128] = low
 
-    def columns(before):
+    def columns(half, before):
         @pl.loop(0, n_y - 1)
         def _(step):
             e = target(step)
             before(e)
-            pack(e)
-            column_start(step, 0)
-            column_start(step, 1)
+            pack(e, half)
+            column_start(half, step, 0)
+            column_start(half, step, 1)
 
         before(y)
-        pack(y)
-        column_start(n_y - 1, 1 - parity)
-        recv[ilev] = send[ilev]
-        recv_scale[ilev] = send_scale[ilev]
+        pack(y, half)
+        column_start(half, n_y - 1, 1 - parity)
+        recv[ilev, half] = send[ilev, half]
+        recv_scale[ilev, half] = send_scale[ilev, half]
+
+    def second_columns(half):
+        columns(
+            half,
+            lambda e: second_part(2 * half, pl.ds(pl.multiple_of(e * width, 128), width)),
+        )
 
     loads[2].wait()
     halo_start(0, 1)
+    tell(ring_one, lev=level(1, parity))
+    tell(ring_one, lev=level(-1, parity))
     for load in loads[3:]:
         load.start()
     for load in loads[:2]:
@@ -401,30 +420,41 @@
         set_coef_y(r)
     pieces(own_part)
     halo_start(4, 5)
-    tell(ring_one, lev=level(1, parity))
-    tell(ring_one, lev=level(-1, parity))
     for load in loads[3:]:
         load.wait()
     write_maps(n_lev, levs, wv, maps)
-    halo_wait(1)
-    first_substep(1)
     pl.semaphore_wait(ring_one, 2)
     tell(ring_two, lev=level(2, parity))
     tell(ring_two, lev=level(-2, parity))
-    halo_wait(0)
-    first_substep(0)
+    is_polar = band_is_polar(ilat)
+    halo_wait(1, 0, 5)
+    first_inner(1)
+    first_outer(1)
+    second_zonal(2)
+    halo_wait(0, 0, 4)
+    first_inner(0)
     pl.semaphore_wait(ring_two, 2)
-    is_polar = jnp.logical_or(ilat < polar, ilat >= n_lat - polar)
+
+    @pl.when(jnp.logical_not(is_polar))
+    def _():
+        second_zonal(0)
+        second_columns(1)
+
+    halo_wait(0, 4, 5)
+    first_outer(0)
+
+    @pl.when(jnp.logical_not(is_polar))
+    def _():
+        second_columns(0)
 
     @pl.when(is_polar)
     def _():
-        pieces(second_part)
+        second_zonal(0)
+        pieces(functools.partial(second_part, 2))
+        pieces(functools.partial(second_part, 0))
         low_pass(u, 0, 0)
-        columns(lambda e: None)
-
-    @pl.when(jnp.logical_not(is_polar))
-    def _():
-        columns(lambda e: second_part(pl.ds(pl.multiple_of(e * width, 128), width)))
+        columns(1, lambda e: None)
+        columns(0, lambda e: None)
 
     for side in (0, 1):
 
@@ -433,24 +463,27 @@
             for copy in halo_copies(side):
                 copy.wait_send()
 
-    column_wait(n_y - 1, 1 - parity)
-    decode(y)
-
-    @pl.loop(1, n_y)
-    def _(lap):
-        step = n_y - 1 - lap
-        column_wait(step, 0)
-        column_wait(step, 1)
-        decode(lax.rem(2 * y + n_y - target(step), n_y))
-
-    @pl.loop(0, n_y - 1)
-    def _(step):
-        for core in range(2):
-            for copy in column_copies(step, core):
-                copy.wait_send()
-
-    for copy in column_copies(n_y - 1, 1 - parity):
-        copy.wait_send()
+    for half in (1, 0):
+        column_wait(half, n_y - 1, 1 - parity)
+        decode(half, y)
+
+        @pl.loop(1, n_y)
+        def _(lap):
+            step = n_y - 1 - lap
+            column_wait(half, step, 0)
+            column_wait(half, step, 1)
+            decode(half, lax.rem(2 * y + n_y - target(step), n_y))
+
+    for half in (1, 0):
+
+        @pl.loop(0, n_y - 1)
+        def _(step):
+            for core in range(2):
+                for copy in column_copies(half, step, core):
+                    copy.wait_send()
+
+        for copy in column_copies(half, n_y - 1, 1 - parity):
+            copy.wait_send()
 
 
 def write_maps(n_lev, levs, wv, maps):
@@ -568,17 +601,17 @@
                 pltpu.VMEM((2, 3, 2 * levs, length), BF16),
                 pltpu.VMEM((2, 3, 2 * levs, length), BF16),
                 pltpu.VMEM((2, 2, levs, length), BF16),
-                pltpu.VMEM((n_lev, tiles, 2 * levs, 128), jnp.int16),
-                pltpu.VMEM((n_lev, tiles, 2 * levs, 128), jnp.int16),
-                pltpu.VMEM((n_lev, 1, 128), F32),
-                pltpu.VMEM((n_lev, 1, 128), F32),
+                pltpu.VMEM((n_lev, 2, tiles // 2, 2 * levs, 128), jnp.int16),
+                pltpu.VMEM((n_lev, 2, tiles // 2, 2 * levs, 128), jnp.int16),
+                pltpu.VMEM((n_lev, 2, 1, 128), F32),
+                pltpu.VMEM((n_lev, 2, 1, 128), F32),
                 dma((9,)),
                 dma((2, 5)),
                 dma((2, 5)),
-                dma((n_lev // 2, 2)),
-                dma((n_lev // 2, 2)),
-                dma((n_lev // 2, 2)),
-                dma((n_lev // 2, 2)),
+                dma((2, n_lev // 2, 2)),
+                dma((2, n_lev // 2, 2)),
+                dma((2, n_lev // 2, 2)),
+                dma((2, n_lev // 2, 2)),
                 pltpu.SemaphoreType.REGULAR,
                 pltpu.SemaphoreType.REGULAR,
             ],

time: 30.2 us -> 30.1 us (level)
  no operation moved by 1% of the time
where the time goes in v7:
time: 30.1 us; the launch traced here: 30 us
  Pallas kernels  29.3 us (97%)
  between operations  0.64 us (2%)
    pallas_call x1, Pallas kernels, shards(): pl.pallas_call(functools.partial(transport, n_lat, n_lev, 16 // rows), na...  27.9 us
    pallas_call x1, Pallas kernels, shards(): pl.pallas_call(remap, name='remap', out_shape=(jax.ShapeDtypeStruct((2, r...  1.43 us

profile of v7, /device:TPU:7, one launch (start us, length us, event | category | flops | bytes accessed | tf_op | source)
XLA Modules:
  0.0 30.0 jit_solution(15039335268032418016)
XLA Ops:
  0.6 27.9 %transport.1 = (bf16[128,768]{1,0:T(8,128)(2,1)S(1)}, bf16[128,768]{1,0:T(8,128)(2,1)S(1)}, bf16[2,192,128]{2,1,0:T(8,128)(2,1)S(1)}, f32[4,384]{1,0:T(4,128)S(1)}) custom-call(f32[2,4,4,3072]{3,2,1,0:T(4,128)} %fields.1, bf16[2,4,4,3072]{3,2,1,0:T(4,128)(2,1)} %courant.1, s32[128]{0:T(128)} %cutoffs.1, f32[4,3072]{1,0:T(4,128)} %surface.1, ...), custom_call_target="tpu_custom_call" | custom-call | tf_op jit(solution)/shard_map/transport/pallas_call | solution.py:574
  28.5 1.4 %remap.1 = (f32[2,4,64,192]{3,2,1,0:T(8,128)}, f32[4,64,192]{2,1,0:T(8,128)}) custom-call(bf16[128,768]{1,0:T(8,128)(2,1)S(1)} %get-tuple-element.6.x_high, bf16[128,768]{1,0:T(8,128)(2,1)S(1)} %get-tuple-element.7.x_low, bf16[2,192,128]{2,1,0:T(8,128)(2,1)S(1)} %get-tuple-element.8.maps, f32[4,384]{1,0:T(4,128)S(1)} %get-tuple-element.9.surf), custom_call_target="tpu_custom_call" | custom-call | tf_op jit(solution)/shard_map/remap/pallas_call | solution.py:623
